TPU v7x, 32 devices: a whole 2x2x4 slice. The times are simulated.
32 devices in a mesh: dp: 2 (over core), expert: 16 (over z, y, x).
Axes of the slice: x: 2, y: 2, z: 4, core: 2. Of those that a mesh axis runs over, the one named last changes fastest.
Arguments:
- tokens: bfloat16 [2048, 2048], P('expert'), may hold values from -6 to 6
- out_grad: bfloat16 [2048, 2048], P('expert'), may hold values from -6 to 6
- route_ids: int32 [2048, 8], P('expert'), may hold values from 0 to 15, all different within a row; in each aligned block of 128 rows (0 to 127, 128 to 255, ...) at most 72 rows name the same one
- route_probs: float32 [2048, 8], P('expert'), may hold values from 0.05 to 1
- gate_store: bfloat16 [16, 2048, 768], P(None, 'expert', 'dp'), may hold values from -0.125 to 0.125
- up_store: bfloat16 [16, 2048, 768], P(None, 'expert', 'dp'), may hold values from -0.125 to 0.125
- down_store: bfloat16 [16, 2048, 768], P(None, 'expert', 'dp'), may hold values from -0.21875 to 0.21875
Outputs:
- grad_gate: bfloat16 [16, 2048, 768], P('expert', None, 'dp')
- grad_up: bfloat16 [16, 2048, 768], P('expert', None, 'dp')
- grad_down: bfloat16 [16, 2048, 768], P('expert', None, 'dp')
- grad_tokens: bfloat16 [2048, 2048], P('expert')
Inputs may be any that keep to these rules, and one draw needn't show every extreme that they name: `route_ids`: among the 128 tokens of one device no expert is named more than 72 times, and in every draw some expert is named exactly 72 times by some device's tokens.
All inputs are finite; a program needn't handle non-finite values.
Results may differ from a plain program's by a relative error of at most 0.0065.
Values may be sent and summed in bfloat16 or wider, within the bound.
A program may use at most 128 MiB of HBM per device.

v0:
```python
import jax
import jax.numpy as jnp
from jax import lax
from jax.sharding import PartitionSpec as P


def joined(own, other):
    first = lax.axis_index("dp") == 0
    return jnp.where(first, jnp.concatenate([own, other], -1), jnp.concatenate([other, own], -1))


def swapped(part):
    return lax.ppermute(part, "dp", [(0, 1), (1, 0)])


def placed(tokens, out_grad, route_ids, route_probs, gate_store, up_store, down_store):
    tok_rows, model_width = tokens.shape
    top_count = route_ids.shape[1]
    experts = lax.axis_size("expert")
    capacity = max(2, 9 * tok_rows * top_count // (8 * experts))
    slots = experts * capacity
    width = model_width // 2
    here = lax.axis_index("dp") * width
    there = width - here
    f32, bf16 = jnp.float32, jnp.bfloat16

    chosen = route_ids[:, :, None] == jnp.arange(experts, dtype=jnp.int32)[None, None, :]
    weight = jnp.sum(jnp.where(chosen, route_probs[:, :, None], 0.0), axis=1)
    named = jnp.any(chosen, axis=1)
    earlier = jnp.arange(tok_rows)[:, None] > jnp.arange(tok_rows)[None, :]
    rank = jnp.dot(earlier.astype(bf16), named.astype(bf16), preferred_element_type=f32)
    rank = jnp.where(named, rank, -1.0)
    hit = rank.T[:, None, :] == jnp.arange(capacity, dtype=f32)[None, :, None]
    slot_prob = jnp.sum(jnp.where(hit, weight.T[:, None, :], 0.0), axis=2)
    place = hit.astype(bf16).reshape(slots, tok_rows)

    x_part = jnp.dot(
        place, lax.dynamic_slice_in_dim(tokens, here, width, 1), preferred_element_type=f32
    ).astype(bf16)
    dy_part = (
        jnp.dot(place, lax.dynamic_slice_in_dim(out_grad, here, width, 1), preferred_element_type=f32)
        * slot_prob.reshape(slots, 1)
    ).astype(bf16)

    def exchange(a):
        return lax.all_to_all(a, "expert", split_axis=0, concat_axis=0, tiled=True)

    def panel(store):
        return lax.all_to_all(store, "expert", split_axis=0, concat_axis=1, tiled=True)[0]

    x_own = exchange(x_part.reshape(experts, capacity, width)).reshape(slots, width)
    gate_panel = panel(gate_store)
    up_panel = panel(up_store)
    dy_own = exchange(dy_part.reshape(experts, capacity, width)).reshape(slots, width)
    down_panel = panel(down_store)
    rows_in = joined(x_own, swapped(x_own))
    dy_rows = joined(dy_own, swapped(dy_own))
    gate_pre = jnp.dot(rows_in, gate_panel, preferred_element_type=f32)
    up_pre = jnp.dot(rows_in, up_panel, preferred_element_type=f32)
    sig = jax.nn.sigmoid(gate_pre)
    activation = (gate_pre * sig * up_pre).astype(bf16)
    act_grad = jnp.dot(dy_rows, down_panel, preferred_element_type=f32)
    up_grad = (act_grad * gate_pre * sig).astype(bf16)
    gate_grad = (act_grad * up_pre * sig * (1.0 + gate_pre * (1.0 - sig))).astype(bf16)
    back = (((1,), (1,)), ((), ()))

    def slot_part(start):
        rows = [lax.dynamic_slice_in_dim(w, start, width, 0) for w in (gate_panel, up_panel)]
        return lax.dot_general(gate_grad, rows[0], back, preferred_element_type=f32) + lax.dot_general(
            up_grad, rows[1], back, preferred_element_type=f32
        )

    arrived = swapped(slot_part(there).astype(bf16))
    summed = (slot_part(here) + arrived.astype(f32)).astype(bf16)
    returned = exchange(summed.reshape(experts, capacity, width)).reshape(slots, width)
    share = lax.dot_general(place, returned, (((0,), (0,)), ((), ())), preferred_element_type=f32).astype(bf16)
    grad_tokens = joined(share, swapped(share))
    outer = (((0,), (0,)), ((), ()))
    grad_down = lax.dot_general(dy_rows, activation, outer, preferred_element_type=f32).astype(bf16)
    grad_gate = lax.dot_general(rows_in, gate_grad, outer, preferred_element_type=f32).astype(bf16)
    grad_up = lax.dot_general(rows_in, up_grad, outer, preferred_element_type=f32).astype(bf16)
    return (grad_gate[None], grad_up[None], grad_down[None], grad_tokens)


def solution(mesh):
    return jax.shard_map(
        placed,
        mesh=mesh,
        in_specs=(
            P("expert", None),
            P("expert", None),
            P("expert", None),
            P("expert", None),
            P(None, "expert", "dp"),
            P(None, "expert", "dp"),
            P(None, "expert", "dp"),
        ),
        out_specs=(
            P("expert", None, "dp"),
            P("expert", None, "dp"),
            P("expert", None, "dp"),
            P("expert", None),
        ),
        check_vma=False,
    )
```

profile of v0, /device:TPU:21, one launch (start us, length us, event | category | flops | bytes accessed | tf_op | source)
XLA Modules:
  0.0 327.1 jit_solution(13981634180581247777)
XLA Ops:
  0.6 40.6 %all_to_all.42 = bf16[16,128,384]{2,1,0:T(8,128)(2,1)} all-to-all(bf16[16,128,384]{2,1,0:T(8,128)(2,1)} %param.11), channel_id=1, replica_groups=mesh['dp'=2,'expert'=16] {'expert'}, dimensions={0} | all-to-all | bytes 3145728 | tf_op jit(solution)/shard_map/all_to_all | solution.py:49
  41.2 7.1 %all-to-all-start.3 = ((bf16[16,128,384]{2,1,0:T(8,128)(2,1)}), bf16[16,128,384]{2,1,0:T(8,128)(2,1)S(1)}, u32[]{:S(2)}, u32[]{:S(2)}) async-start(bf16[16,128,384]{2,1,0:T(8,128)(2,1)} %param.12), calls=%async_computation.3 | async-start | bytes 3145728 | tf_op jit(solution)/shard_map/all_to_all | solution.py:49
  48.6 0.2 bitcast_compare_fusion
  48.8 2.2 convolution_convert_fusion
  51.0 31.9 %all-to-all-done.3 = bf16[16,128,384]{2,1,0:T(8,128)(2,1)S(1)} async-done(((bf16[16,128,384]{2,1,0:T(8,128)(2,1)}), bf16[16,128,384]{2,1,0:T(8,128)(2,1)S(1)}, u32[]{:S(2)}, u32[]{:S(2)}) %all-to-all-start.3) | async-done | bytes 1572896 | tf_op jit(solution)/shard_map/all_to_all | solution.py:49
  82.9 6.5 %all-to-all-start = ((bf16[16,72,1024]{2,1,0:T(8,128)(2,1)}), bf16[16,72,1024]{2,1,0:T(8,128)(2,1)}, u32[]{:S(2)}, u32[]{:S(2)}) async-start(bf16[16,72,1024]{2,1,0:T(8,128)(2,1)} %bitcast.2), calls=%async_computation | async-start | bytes 4718592 | tf_op jit(solution)/shard_map/all_to_all | solution.py:46
  89.4 0.3 select_reduce_fusion
  89.9 2.2 fusion
  92.2 48.3 %all-to-all-done = bf16[16,72,1024]{2,1,0:T(8,128)(2,1)} async-done(((bf16[16,72,1024]{2,1,0:T(8,128)(2,1)}), bf16[16,72,1024]{2,1,0:T(8,128)(2,1)}, u32[]{:S(2)}, u32[]{:S(2)}) %all-to-all-start) | async-done | bytes 2359328 | tf_op jit(solution)/shard_map/all_to_all | solution.py:46
  140.5 6.5 %all-to-all-start.1 = ((bf16[16,72,1024]{2,1,0:T(8,128)(2,1)}), bf16[16,72,1024]{2,1,0:T(8,128)(2,1)}, u32[]{:S(2)}, u32[]{:S(2)}) async-start(bf16[16,72,1024]{2,1,0:T(8,128)(2,1)} %bitcast.5), calls=%async_computation.1 | async-start | bytes 4718592 | tf_op jit(solution)/shard_map/all_to_all | solution.py:46
  147.0 2.2 collective-permute-start
  149.2 49.0 %all-to-all-done.1 = bf16[16,72,1024]{2,1,0:T(8,128)(2,1)} async-done(((bf16[16,72,1024]{2,1,0:T(8,128)(2,1)}), bf16[16,72,1024]{2,1,0:T(8,128)(2,1)}, u32[]{:S(2)}, u32[]{:S(2)}) %all-to-all-start.1) | async-done | bytes 2359328 | tf_op jit(solution)/shard_map/all_to_all | solution.py:46
  198.1 6.5 %all-to-all-start.2 = ((bf16[16,128,384]{2,1,0:T(8,128)(2,1)}), bf16[16,128,384]{2,1,0:T(8,128)(2,1)}, u32[]{:S(2)}, u32[]{:S(2)}) async-start(bf16[16,128,384]{2,1,0:T(8,128)(2,1)} %param.13), calls=%async_computation.2 | async-start | bytes 3145728 | tf_op jit(solution)/shard_map/all_to_all | solution.py:49
  204.6 2.2 collective-permute-start.1
  206.8 8.1 %fusion.29 = f32[1152,384]{1,0:T(8,128)} fusion(bf16[2048,384]{1,0:T(8,128)(2,1)} %bitcast.40, bf16[1152,1024]{1,0:T(8,128)(2,1)} %collective-permute-done, bf16[1152,1024]{1,0:T(8,128)(2,1)} %bitcast.3, pred[]{:T(512)S(6)} %eq.42), kind=kOutput, calls=%fused_computation.50 | convolution fusion | flops 1833172992 | bytes 8060929 | tf_op jit(solution)/shard_map/dot_general | solution.py:58
  214.9 7.6 %fusion.30 = f32[1152,384]{1,0:T(8,128)} fusion(bf16[2048,384]{1,0:T(8,128)(2,1)S(1)} %bitcast.37, bf16[1152,1024]{1,0:T(8,128)(2,1)} %collective-permute-done, bf16[1152,1024]{1,0:T(8,128)(2,1)} %bitcast.3, pred[]{:T(512)S(6)} %eq.42), kind=kOutput, calls=%fused_computation.51 | convolution fusion | flops 1833172992 | bytes 8060929 | tf_op jit(solution)/shard_map/dot_general | solution.py:59
  222.5 16.2 %all-to-all-done.2 = bf16[16,128,384]{2,1,0:T(8,128)(2,1)} async-done(((bf16[16,128,384]{2,1,0:T(8,128)(2,1)}), bf16[16,128,384]{2,1,0:T(8,128)(2,1)}, u32[]{:S(2)}, u32[]{:S(2)}) %all-to-all-start.2) | async-done | bytes 1572896 | tf_op jit(solution)/shard_map/all_to_all | solution.py:49
  238.7 7.5 %multiply_convert_fusion.1 = (bf16[1152,384]{1,0:T(8,128)(2,1)S(1)}, bf16[1152,384]{1,0:T(8,128)(2,1)S(1)}) fusion(f32[1152,384]{1,0:T(8,128)} %fusion.29, f32[1152,384]{1,0:T(8,128)} %fusion.30, bf16[2048,384]{1,0:T(8,128)(2,1)} %bitcast.7, bf16[1152,1024]{1,0:T(8,128)(2,1)} %collective-permute-done.1, bf16[1152,1024]{1,0:T(8,128)(2,1)} %bitcast.6, ...), kind=kOutput, calls=%fused_computation.16 | convolution fusion | flops 1838923776 | bytes 11599873 | tf_op jit(solution)/shard_map/dot_general | solution.py:62
  246.2 1.4 fusion.9
  247.7 1.5 fusion.1
  249.1 1.5 collective-permute-start.2
  250.6 1.4 fusion.14
  252.0 2.7 collective-permute-done.2
  254.7 2.9 add_convert_fusion
  257.7 6.9 %all-to-all-start.5 = ((bf16[16,72,1024]{2,1,0:T(8,128)(2,1)}), bf16[16,72,1024]{2,1,0:T(8,128)(2,1)S(1)}, u32[]{:S(2)}, u32[]{:S(2)}) async-start(bf16[16,72,1024]{2,1,0:T(8,128)(2,1)} %bitcast.36), calls=%async_computation.5 | async-start | bytes 4718592 | tf_op jit(solution)/shard_map/all_to_all | solution.py:46
  264.6 8.1 %fusion.3 = bf16[1,2048,384]{2,1,0:T(8,128)(2,1)} fusion(bf16[1152,384]{1,0:T(8,128)(2,1)} %copy-done.4, bf16[1152,1024]{1,0:T(8,128)(2,1)} %collective-permute-done, bf16[1152,1024]{1,0:T(8,128)(2,1)} %bitcast.3, pred[]{:T(512)S(6)} %eq.42), kind=kOutput, calls=%fused_computation.13 | convolution fusion | flops 1833959424 | bytes 7176193 | tf_op jit(solution)/shard_map/dot_general | solution.py:81
  272.8 8.1 %fusion.4 = bf16[1,2048,384]{2,1,0:T(8,128)(2,1)} fusion(f32[1152,384]{1,0:T(8,128)S(1)} %copy-done.9, f32[1152,384]{1,0:T(8,128)S(1)} %copy-done.8, bf16[1152,1024]{1,0:T(8,128)(2,1)} %collective-permute-done.1, bf16[1152,1024]{1,0:T(8,128)(2,1)} %bitcast.6, pred[]{:T(512)S(6)} %eq.42), kind=kOutput, calls=%fused_computation.14 | convolution fusion | flops 1836613632 | bytes 9830401 | tf_op jit(solution)/shard_map/dot_general | solution.py:79
  280.8 35.5 %all-to-all-done.5 = bf16[16,72,1024]{2,1,0:T(8,128)(2,1)S(1)} async-done(((bf16[16,72,1024]{2,1,0:T(8,128)(2,1)}), bf16[16,72,1024]{2,1,0:T(8,128)(2,1)S(1)}, u32[]{:S(2)}, u32[]{:S(2)}) %all-to-all-start.5) | async-done | bytes 2359328 | tf_op jit(solution)/shard_map/all_to_all | solution.py:46
  316.3 0.6 fusion.5
  316.9 1.5 collective-permute-start.3
  318.3 7.8 %fusion.2 = bf16[1,2048,384]{2,1,0:T(8,128)(2,1)} fusion(bf16[1152,384]{1,0:T(8,128)(2,1)S(1)} %copy-done.2, bf16[1152,1024]{1,0:T(8,128)(2,1)} %collective-permute-done, bf16[1152,1024]{1,0:T(8,128)(2,1)} %bitcast.3, pred[]{:T(512)S(6)} %eq.42), kind=kOutput, calls=%fused_computation.12 | convolution fusion | flops 1833959424 | bytes 7176193 | tf_op jit(solution)/shard_map/dot_general | solution.py:80
  326.2 0.9 maximum_select_fusion.4
  (29 shorter events, 0.4 us)
Async XLA Ops:
  0.6 48.2 %copy-start = (bf16[128,2048]{1,0:T(8,128)(2,1)S(1)}, bf16[128,2048]{1,0:T(8,128)(2,1)}, u32[]{:S(2)}) copy-start(bf16[128,2048]{1,0:T(8,128)(2,1)} %param.7) | copy-start | bytes 1572868
  41.2 7.2 %copy-start.6 = (s32[128,8]{0,1:T(8,128)S(1)}, s32[128,8]{0,1:T(8,128)}, u32[]{:S(2)}) copy-start(s32[128,8]{0,1:T(8,128)} %param.9) | copy-start | bytes 12292
  41.2 41.7 %all-to-all-start.3 = ((bf16[16,128,384]{2,1,0:T(8,128)(2,1)}), bf16[16,128,384]{2,1,0:T(8,128)(2,1)S(1)}, u32[]{:S(2)}, u32[]{:S(2)}) async-start(bf16[16,128,384]{2,1,0:T(8,128)(2,1)} %param.12), calls=%async_computation.3 | async-start | bytes 3145728 | tf_op jit(solution)/shard_map/all_to_all | solution.py:49
  82.9 6.5 %copy-start.7 = (f32[128,8]{0,1:T(8,128)S(1)}, f32[128,8]{0,1:T(8,128)}, u32[]{:S(2)}) copy-start(f32[128,8]{0,1:T(8,128)} %param.10) | copy-start | bytes 12292
  82.9 7.0 %copy-start.5 = (bf16[128,2048]{1,0:T(8,128)(2,1)S(1)}, bf16[128,2048]{1,0:T(8,128)(2,1)}, u32[]{:S(2)}) copy-start(bf16[128,2048]{1,0:T(8,128)(2,1)} %param.8) | copy-start | bytes 1572868
  82.9 57.6 %all-to-all-start = ((bf16[16,72,1024]{2,1,0:T(8,128)(2,1)}), bf16[16,72,1024]{2,1,0:T(8,128)(2,1)}, u32[]{:S(2)}, u32[]{:S(2)}) async-start(bf16[16,72,1024]{2,1,0:T(8,128)(2,1)} %bitcast.2), calls=%async_computation | async-start | bytes 4718592 | tf_op jit(solution)/shard_map/all_to_all | solution.py:46
  140.5 57.6 %all-to-all-start.1 = ((bf16[16,72,1024]{2,1,0:T(8,128)(2,1)}), bf16[16,72,1024]{2,1,0:T(8,128)(2,1)}, u32[]{:S(2)}, u32[]{:S(2)}) async-start(bf16[16,72,1024]{2,1,0:T(8,128)(2,1)} %bitcast.5), calls=%async_computation.1 | async-start | bytes 4718592 | tf_op jit(solution)/shard_map/all_to_all | solution.py:46
  147.0 59.8 %collective-permute-start = (bf16[1152,1024]{1,0:T(8,128)(2,1)}, bf16[1152,1024]{1,0:T(8,128)(2,1)}, u32[]{:S(2)}, u32[]{:S(2)}) collective-permute-start(bf16[1152,1024]{1,0:T(8,128)(2,1)} %bitcast.3), channel_id=1, source_target_pairs={{0,16},{16,0},{1,17},{17,1},{2,18},{18,2},{3,19},{19,3},{4,20},{20... | collective-permute-start | bytes 7077896 | tf_op jit(solution)/shard_map/ppermute | solution.py:13
  198.1 40.5 %all-to-all-start.2 = ((bf16[16,128,384]{2,1,0:T(8,128)(2,1)}), bf16[16,128,384]{2,1,0:T(8,128)(2,1)}, u32[]{:S(2)}, u32[]{:S(2)}) async-start(bf16[16,128,384]{2,1,0:T(8,128)(2,1)} %param.13), calls=%async_computation.2 | async-start | bytes 3145728 | tf_op jit(solution)/shard_map/all_to_all | solution.py:49
  204.6 34.1 %collective-permute-start.1 = (bf16[1152,1024]{1,0:T(8,128)(2,1)}, bf16[1152,1024]{1,0:T(8,128)(2,1)}, u32[]{:S(2)}, u32[]{:S(2)}) collective-permute-start(bf16[1152,1024]{1,0:T(8,128)(2,1)} %bitcast.6), channel_id=1, source_target_pairs={{0,16},{16,0},{1,17},{17,1},{2,18},{18,2},{3,19},{19,3},{4,20},{20... | collective-permute-start | bytes 7077896 | tf_op jit(solution)/shard_map/ppermute | solution.py:13
  238.7 7.5 %copy-start.3 = (bf16[16,128,384]{2,1,0:T(8,128)(2,1)S(1)}, bf16[16,128,384]{2,1,0:T(8,128)(2,1)}, u32[]{:S(2)}) copy-start(bf16[16,128,384]{2,1,0:T(8,128)(2,1)} %all_to_all.42) | copy-start | bytes 4718596
  246.2 4.4 %copy-start.1 = (bf16[1152,384]{1,0:T(8,128)(2,1)}, bf16[1152,384]{1,0:T(8,128)(2,1)S(1)}, u32[]{:S(2)}) copy-start(bf16[1152,384]{1,0:T(8,128)(2,1)S(1)} %get-tuple-element.5) | copy-start | bytes 2654212
  246.2 8.5 %copy-start.4 = (bf16[1152,384]{1,0:T(8,128)(2,1)}, bf16[1152,384]{1,0:T(8,128)(2,1)S(1)}, u32[]{:S(2)}) copy-start(bf16[1152,384]{1,0:T(8,128)(2,1)S(1)} %get-tuple-element.4) | copy-start | bytes 2654212
  249.1 5.6 %collective-permute-start.2 = (bf16[1152,1024]{1,0:T(8,128)(2,1)S(1)}, bf16[1152,1024]{1,0:T(8,128)(2,1)S(1)}, u32[]{:S(2)}, u32[]{:S(2)}) collective-permute-start(bf16[1152,1024]{1,0:T(8,128)(2,1)S(1)} %fusion.1), channel_id=1, source_target_pairs={{0,16},{16,0},{1,17},{17,1},{2,18},{18,2},{3,19},{19,3},{4,20},{20... | collective-permute-start | bytes 7077896 | tf_op jit(solution)/shard_map/ppermute | solution.py:13
  257.7 58.6 %all-to-all-start.5 = ((bf16[16,72,1024]{2,1,0:T(8,128)(2,1)}), bf16[16,72,1024]{2,1,0:T(8,128)(2,1)S(1)}, u32[]{:S(2)}, u32[]{:S(2)}) async-start(bf16[16,72,1024]{2,1,0:T(8,128)(2,1)} %bitcast.36), calls=%async_computation.5 | async-start | bytes 4718592 | tf_op jit(solution)/shard_map/all_to_all | solution.py:46
  264.6 8.2 %copy-start.8 = (f32[1152,384]{1,0:T(8,128)S(1)}, f32[1152,384]{1,0:T(8,128)}, u32[]{:S(2)}) copy-start(f32[1152,384]{1,0:T(8,128)} %fusion.29) | copy-start | bytes 5308420
  264.6 8.2 %copy-start.9 = (f32[1152,384]{1,0:T(8,128)S(1)}, f32[1152,384]{1,0:T(8,128)}, u32[]{:S(2)}) copy-start(f32[1152,384]{1,0:T(8,128)} %fusion.30) | copy-start | bytes 5308420
  316.3 2.0 copy-start.2
  316.9 9.3 %collective-permute-start.3 = (bf16[128,1024]{1,0:T(8,128)(2,1)S(1)}, bf16[128,1024]{1,0:T(8,128)(2,1)S(1)}, u32[]{:S(2)}, u32[]{:S(2)}) collective-permute-start(bf16[128,1024]{1,0:T(8,128)(2,1)S(1)} %fusion.5), channel_id=1, source_target_pairs={{0,16},{16,0},{1,17},{17,1},{2,18},{18,2},{3,19},{19,3},{4,20},{20... | collective-permute-start | bytes 786440 | tf_op jit(solution)/shard_map/ppermute | solution.py:13
where the time goes:
time: 330 us; the launch traced here: 327 us
  waiting for transfers between devices  184 us (56%)
  matrix products  59.6 us (18%)
  starting transfers between devices  40.7 us (12%)
  blocking collectives  40.6 us (12%)
    all_to_all x3, waiting for transfers between devices, exchange(): return lax.all_to_all(a, 'expert', split_axis=0, concat_axis=0, tiled=True)  133 us
    all_to_all x2, waiting for transfers between devices, panel(): lax.all_to_all(store, 'expert', split_axis=0, concat_axis=1, tiled=True)[0]  48.1 us
    all_to_all x1, blocking collectives, panel(): lax.all_to_all(store, 'expert', split_axis=0, concat_axis=1, tiled=True)[0]  40.6 us
    all_to_all x3, starting transfers between devices, exchange(): return lax.all_to_all(a, 'expert', split_axis=0, concat_axis=0, tiled=True)  19.9 us
    all_to_all x2, starting transfers between devices, panel(): lax.all_to_all(store, 'expert', split_axis=0, concat_axis=1, tiled=True)[0]  13.6 us
    dot_general x1, matrix products, placed(): lax.dot_general(rows_in, up_grad, outer, preferred_element_type=f32)  8.14 us
    dot_general x1, matrix products, placed(): gate_pre = jnp.dot(rows_in, gate_panel, preferred_element_type=f32)  8.1 us
    dot_general x1, matrix products, placed(): lax.dot_general(dy_rows, activation, outer, preferred_element_type=f32)  8.06 us
  transfers between devices with their start and end apart: 9, of which 6 were waited for; matrix products, arithmetic and copies ran while one was open for 14% of the time, Pallas kernels for 0%

commit v1 on v0

--- a/solution.py
+++ b/solution.py
@@ -13,7 +13,7 @@
     return lax.ppermute(part, "dp", [(0, 1), (1, 0)])
 
 
-def placed(tokens, out_grad, route_ids, route_probs, gate_store, up_store, down_store):
+def placed_sparse(tokens, out_grad, route_ids, route_probs, gate_store, up_store, down_store):
     tok_rows, model_width = tokens.shape
     top_count = route_ids.shape[1]
     experts = lax.axis_size("expert")
@@ -82,6 +82,79 @@
     return (grad_gate[None], grad_up[None], grad_down[None], grad_tokens)
 
 
+def placed_dense(tokens, out_grad, route_ids, route_probs, gate_store, up_store, down_store):
+    tok_rows, model_width = tokens.shape
+    top_count = route_ids.shape[1]
+    experts = lax.axis_size("expert")
+    capacity = max(2, 9 * tok_rows * top_count // (8 * experts))
+    slots = experts * capacity
+    width = model_width // 2
+    here = lax.axis_index("dp") * width
+    there = width - here
+    me = lax.axis_index("expert")
+    f32, bf16 = jnp.float32, jnp.bfloat16
+
+    def panel(store):
+        return lax.all_to_all(store, "expert", split_axis=0, concat_axis=1, tiled=True)[0]
+
+    route = jnp.concatenate([route_ids.astype(f32), route_probs], axis=1)
+    route = lax.all_gather(route, "expert", axis=0, tiled=False)
+    x_all = lax.all_gather(lax.dynamic_slice_in_dim(tokens, here, width, 1), "expert", axis=0, tiled=False)
+    dy_all = lax.all_gather(lax.dynamic_slice_in_dim(out_grad, here, width, 1), "expert", axis=0, tiled=False)
+    chosen = route[:, :, :top_count] == me.astype(f32)
+    weight = jnp.sum(jnp.where(chosen, route[:, :, top_count:], 0.0), axis=2)
+    named = jnp.any(chosen, axis=2)
+    earlier = jnp.arange(tok_rows)[:, None] < jnp.arange(tok_rows)[None, :]
+    rank = jnp.dot(named.astype(bf16), earlier.astype(bf16), preferred_element_type=f32)
+    rank = jnp.where(named, rank, -1.0)
+    hit = rank[:, None, :] == jnp.arange(capacity, dtype=f32)[None, :, None]
+    slot_prob = jnp.sum(jnp.where(hit, weight[:, None, :], 0.0), axis=2)
+    place = hit.astype(bf16)
+    batch = (((2,), (1,)), ((0,), (0,)))
+    x_own = lax.dot_general(place, x_all, batch, preferred_element_type=f32).astype(bf16).reshape(slots, width)
+    dy_own = (
+        lax.dot_general(place, dy_all, batch, preferred_element_type=f32) * slot_prob[:, :, None]
+    ).astype(bf16).reshape(slots, width)
+    gate_panel = panel(gate_store)
+    up_panel = panel(up_store)
+    down_panel = panel(down_store)
+    rows_in = joined(x_own, swapped(x_own))
+    dy_rows = joined(dy_own, swapped(dy_own))
+    gate_pre = jnp.dot(rows_in, gate_panel, preferred_element_type=f32)
+    up_pre = jnp.dot(rows_in, up_panel, preferred_element_type=f32)
+    sig = jax.nn.sigmoid(gate_pre)
+    activation = (gate_pre * sig * up_pre).astype(bf16)
+    act_grad = jnp.dot(dy_rows, down_panel, preferred_element_type=f32)
+    up_grad = (act_grad * gate_pre * sig).astype(bf16)
+    gate_grad = (act_grad * up_pre * sig * (1.0 + gate_pre * (1.0 - sig))).astype(bf16)
+    back = (((1,), (1,)), ((), ()))
+
+    def slot_part(start):
+        rows = [lax.dynamic_slice_in_dim(w, start, width, 0) for w in (gate_panel, up_panel)]
+        return lax.dot_general(gate_grad, rows[0], back, preferred_element_type=f32) + lax.dot_general(
+            up_grad, rows[1], back, preferred_element_type=f32
+        )
+
+    arrived = swapped(slot_part(there).astype(bf16))
+    summed = (slot_part(here) + arrived.astype(f32)).astype(bf16)
+    sums = lax.dot_general(
+        place, summed.reshape(experts, capacity, width), (((1,), (1,)), ((0,), (0,))), preferred_element_type=f32
+    ).astype(bf16)
+    share = lax.psum_scatter(sums, "expert", scatter_dimension=0, tiled=False)
+    grad_tokens = joined(share, swapped(share))
+    outer = (((0,), (0,)), ((), ()))
+    grad_down = lax.dot_general(dy_rows, activation, outer, preferred_element_type=f32).astype(bf16)
+    grad_gate = lax.dot_general(rows_in, gate_grad, outer, preferred_element_type=f32).astype(bf16)
+    grad_up = lax.dot_general(rows_in, up_grad, outer, preferred_element_type=f32).astype(bf16)
+    return (grad_gate[None], grad_up[None], grad_down[None], grad_tokens)
+
+
+def placed(tokens, out_grad, route_ids, route_probs, gate_store, up_store, down_store):
+    dense = 4 * route_ids.shape[1] >= lax.axis_size("expert")
+    body = placed_dense if dense else placed_sparse
+    return body(tokens, out_grad, route_ids, route_probs, gate_store, up_store, down_store)
+
+
 def solution(mesh):
     return jax.shard_map(
         placed,

time: 330 us -> 378 us (1.15)
  blocking collectives: 40.6 us -> 131 us
  waiting for transfers between devices: 184 us -> 139 us
  starting transfers between devices: 40.7 us -> 19.9 us
  between operations: 0.79 us -> 13.9 us
  matrix products: 59.6 us -> 65.6 us
    all_to_all x3 -> x0, waiting for transfers between devices: 133 us -> none  [exchange(): return lax.all_to_all(a, 'expert', split_axis=0, concat_axis=0, tiled=True)]
    reduce_scatter x0 -> x1, waiting for transfers between devices: none -> 78.8 us  [placed_dense(): share = lax.psum_scatter(sums, 'expert', scatter_dimension=0, tiled=False)]
    all_gather x0 -> x1, blocking collectives: none -> 73.5 us  [placed_dense(): route = lax.all_gather(route, 'expert', axis=0, tiled=False)]
    all_gather x0 -> x2, waiting for transfers between devices: none -> 57.6 us  [the longest x1 57.6 us: placed_dense(): lax.all_gather(lax.dynamic_slice_in_dim(out_grad, here, width, 1), 'exper...]
    all_to_all x2, waiting for transfers between devices: 48.1 us -> 0.01 us  [panel(): lax.all_to_all(store, 'expert', split_axis=0, concat_axis=1, tiled=True)[0]]
    all_to_all x3 -> x0, starting transfers between devices: 19.9 us -> none  [exchange(): return lax.all_to_all(a, 'expert', split_axis=0, concat_axis=0, tiled=True)]
    all_to_all x1, blocking collectives: 40.6 us -> 57.2 us  [panel(): lax.all_to_all(store, 'expert', split_axis=0, concat_axis=1, tiled=True)[0]]
    dot_general x10, matrix products: 52.4 us -> 59.7 us  [the longest x1 8.22 us: placed_dense(): lax.dot_general(dy_rows, activation, outer, preferred_element_type=f32)]
  transfers between devices with their start and end apart: 9 -> 9, of which waited for: 6 -> 3; matrix products, arithmetic and copies ran while one was open for 14% -> 14% of each run, Pallas kernels for 0% -> 0%
where the time goes in v1:
time: 378 us; the launch traced here: 374 us
  waiting for transfers between devices  139 us (37%)
  blocking collectives  131 us (35%)
  matrix products  65.6 us (17%)
  starting transfers between devices  19.9 us (5%)
  between operations  13.9 us (4%)
    reduce_scatter x1, waiting for transfers between devices, placed_dense(): share = lax.psum_scatter(sums, 'expert', scatter_dimension=0, tiled=False)  78.8 us
    all_gather x1, blocking collectives, placed_dense(): route = lax.all_gather(route, 'expert', axis=0, tiled=False)  73.5 us
    all_gather x1, waiting for transfers between devices, placed_dense(): lax.all_gather(lax.dynamic_slice_in_dim(out_grad, here, width, 1), 'exper...  57.6 us
    all_to_all x1, blocking collectives, panel(): lax.all_to_all(store, 'expert', split_axis=0, concat_axis=1, tiled=True)[0]  57.2 us
    all_to_all x2, starting transfers between devices, panel(): lax.all_to_all(store, 'expert', split_axis=0, concat_axis=1, tiled=True)[0]  12.5 us
    dot_general x1, matrix products, placed_dense(): lax.dot_general(dy_rows, activation, outer, preferred_element_type=f32)  8.22 us
    dot_general x1, matrix products, placed_dense(): lax.dot_general(rows_in, gate_grad, outer, preferred_element_type=f32)  8.03 us
    dot_general x1, matrix products, placed_dense(): gate_pre = jnp.dot(rows_in, gate_panel, preferred_element_type=f32)  8.01 us
  transfers between devices with their start and end apart: 9, of which 3 were waited for; matrix products, arithmetic and copies ran while one was open for 14% of the time, Pallas kernels for 0%

profile of v1, /device:TPU:21, one launch (start us, length us, event | category | flops | bytes accessed | tf_op | source)
XLA Modules:
  0.0 374.4 jit_solution(1675728616355663921)
XLA Ops:
  7.2 0.0 all-gather.6.cloned.1.call-start
  7.3 1.0 copy-done
  8.2 0.7 constant_dynamic-slice_fusion.1
  9.0 0.0 all-gather.8.cloned.1.call-start
  9.0 1.7 constant_dynamic-slice_fusion
  10.7 57.2 %all_to_all.12 = bf16[16,128,384]{2,1,0:T(8,128)(2,1)} all-to-all(bf16[16,128,384]{2,1,0:T(8,128)(2,1)} %param.11), channel_id=1, replica_groups=mesh['dp'=2,'expert'=16] {'expert'}, dimensions={0} | all-to-all | bytes 3145728 | tf_op jit(solution)/shard_map/all_to_all | solution.py:98
  67.9 7.0 %all-to-all-start.1 = ((bf16[16,128,384]{2,1,0:T(8,128)(2,1)}), bf16[16,128,384]{2,1,0:T(8,128)(2,1)S(1)}, u32[]{:S(2)}, u32[]{:S(2)}) async-start(bf16[16,128,384]{2,1,0:T(8,128)(2,1)} %param.12), calls=%async_computation.1 | async-start | bytes 3145728 | tf_op jit(solution)/shard_map/all_to_all | solution.py:98
  74.9 73.5 %all-gather = f32[2048,16]{0,1:T(8,128)S(1)} all-gather(f32[128,16]{0,1:T(8,128)S(1)} %pad_maximum_fusion), channel_id=2, replica_groups=mesh['dp'=2,'expert'=16] {'expert'}, dimensions={0}, use_global_device_ids=true | all-gather | bytes 139264 | tf_op jit(solution)/shard_map/all_gather | solution.py:101
  148.6 0.1 convolution_select_fusion
  148.7 4.4 %convolution_convert_fusion.4 = bf16[16,72,1024]{2,1,0:T(8,128)(2,1)} fusion(bf16[16,128,1024]{2,1,0:T(8,128)(2,1)} %bitcast.39, f32[16,128]{1,0:T(8,128)S(1)} %convolution_select_fusion), kind=kOutput, calls=%fused_computation.14 | convolution fusion | flops 303316992 | bytes 6561792 | tf_op jit(solution)/shard_map/dot_general | solution.py:114
  153.1 6.2 %collective-permute-start = (bf16[1152,1024]{1,0:T(8,128)(2,1)}, bf16[1152,1024]{1,0:T(8,128)(2,1)}, u32[]{:S(2)}, u32[]{:S(2)}) collective-permute-start(bf16[1152,1024]{1,0:T(8,128)(2,1)} %bitcast.1), channel_id=1, source_target_pairs={{0,16},{16,0},{1,17},{17,1},{2,18},{18,2},{3,19},{19,3},{4,20},{20... | collective-permute-start | bytes 7077896 | tf_op jit(solution)/shard_map/ppermute | solution.py:13
  159.3 5.6 %all-to-all-start = ((bf16[16,128,384]{2,1,0:T(8,128)(2,1)}), bf16[16,128,384]{2,1,0:T(8,128)(2,1)}, u32[]{:S(2)}, u32[]{:S(2)}) async-start(bf16[16,128,384]{2,1,0:T(8,128)(2,1)} %param.13), calls=%async_computation | async-start | bytes 3145728 | tf_op jit(solution)/shard_map/all_to_all | solution.py:98
  164.9 0.3 select_reduce_fusion
  165.3 57.6 %all-gather.8.cloned.1.call-done = bf16[2048,1024]{1,0:T(8,128)(2,1)} async-done(((bf16[128,1024]{1,0:T(8,128)(2,1)}), bf16[2048,1024]{1,0:T(8,128)(2,1)}) %all-gather.8.cloned.1.call-update) | async-done | bytes 4194320 | tf_op jit(solution)/shard_map/all_gather | solution.py:103
  222.9 4.4 %multiply_convert_fusion = bf16[16,72,1024]{2,1,0:T(8,128)(2,1)} fusion(f32[16,72]{1,0:T(8,128)S(1)} %select_reduce_fusion, bf16[16,128,1024]{2,1,0:T(8,128)(2,1)} %bitcast.40, f32[16,128]{1,0:T(8,128)S(1)} %convolution_select_fusion), kind=kOutput, calls=%fused_computation.5 | convolution fusion | flops 304496640 | bytes 6566400 | tf_op jit(solution)/shard_map/dot_general | solution.py:116
  227.3 0.4 collective-permute-start.1
  227.7 8.0 %fusion.25 = f32[1152,384]{1,0:T(8,128)} fusion(bf16[2048,384]{1,0:T(8,128)(2,1)} %bitcast.36, bf16[1152,1024]{1,0:T(8,128)(2,1)} %collective-permute-done, bf16[1152,1024]{1,0:T(8,128)(2,1)} %bitcast.1, pred[]{:T(512)S(6)} %eq.24), kind=kOutput, calls=%fused_computation.48 | convolution fusion | flops 1833172992 | bytes 8060929 | tf_op jit(solution)/shard_map/dot_general | solution.py:123
  235.7 7.6 %fusion.26 = f32[1152,384]{1,0:T(8,128)} fusion(bf16[2048,384]{1,0:T(8,128)(2,1)S(1)} %bitcast.33, bf16[1152,1024]{1,0:T(8,128)(2,1)} %collective-permute-done, bf16[1152,1024]{1,0:T(8,128)(2,1)} %bitcast.1, pred[]{:T(512)S(6)} %eq.24), kind=kOutput, calls=%fused_computation.49 | convolution fusion | flops 1833172992 | bytes 8060929 | tf_op jit(solution)/shard_map/dot_general | solution.py:124
  243.4 7.6 %multiply_convert_fusion.2 = (bf16[1152,384]{1,0:T(8,128)(2,1)S(1)}, bf16[1152,384]{1,0:T(8,128)(2,1)S(1)}) fusion(f32[1152,384]{1,0:T(8,128)} %fusion.25, f32[1152,384]{1,0:T(8,128)} %fusion.26, bf16[2048,384]{1,0:T(8,128)(2,1)} %bitcast.4, bf16[1152,1024]{1,0:T(8,128)(2,1)} %collective-permute-done.1, bf16[1152,1024]{1,0:T(8,128)(2,1)} %bitcast.3, ...), kind=kOutput, calls=%fused_computation.16 | convolution fusion | flops 1838923776 | bytes 11599873 | tf_op jit(solution)/shard_map/dot_general | solution.py:127
  251.0 1.4 fusion.7
  252.4 1.5 fusion
  253.9 0.1 collective-permute-start.2
  254.0 1.4 fusion.12
  255.4 3.0 collective-permute-done.2
  258.5 1.5 add_convert_fusion
  260.0 3.4 convolution_convert_fusion.3
  263.5 8.0 %fusion.2 = bf16[1,2048,384]{2,1,0:T(8,128)(2,1)} fusion(bf16[1152,384]{1,0:T(8,128)(2,1)S(1)} %copy-done.3, bf16[1152,1024]{1,0:T(8,128)(2,1)} %collective-permute-done, bf16[1152,1024]{1,0:T(8,128)(2,1)} %bitcast.1, pred[]{:T(512)S(6)} %eq.24), kind=kOutput, calls=%fused_computation.12 | convolution fusion | flops 1833959424 | bytes 7176193 | tf_op jit(solution)/shard_map/dot_general | solution.py:148
  271.4 8.2 %fusion.3 = bf16[1,2048,384]{2,1,0:T(8,128)(2,1)} fusion(f32[1152,384]{1,0:T(8,128)S(1)} %copy-done.8, f32[1152,384]{1,0:T(8,128)S(1)} %copy-done.7, bf16[1152,1024]{1,0:T(8,128)(2,1)} %collective-permute-done.1, bf16[1152,1024]{1,0:T(8,128)(2,1)} %bitcast.3, pred[]{:T(512)S(6)} %eq.24), kind=kOutput, calls=%fused_computation.13 | convolution fusion | flops 1836613632 | bytes 9830401 | tf_op jit(solution)/shard_map/dot_general | solution.py:146
  279.7 78.8 %reduce-scatter.2.cloned.1.call-done = bf16[1,128,1024]{2,1,0:T(8,128)(2,1)} async-done(((bf16[16,128,1024]{2,1,0:T(8,128)(2,1)}), bf16[1,128,1024]{2,1,0:T(8,128)(2,1)}) %reduce-scatter.2.cloned.1.call-update) | async-done | bytes 262160 | tf_op jit(solution)/shard_map/reduce_scatter | solution.py:143
  358.5 0.4 collective-permute-start.3
  358.9 8.0 %fusion.1 = bf16[1,2048,384]{2,1,0:T(8,128)(2,1)} fusion(bf16[1152,384]{1,0:T(8,128)(2,1)S(1)} %get-tuple-element.7, bf16[1152,1024]{1,0:T(8,128)(2,1)} %collective-permute-done, bf16[1152,1024]{1,0:T(8,128)(2,1)} %bitcast.1, pred[]{:T(512)S(6)} %eq.24), kind=kOutput, calls=%fused_computation.11 | convolution fusion | flops 1833959424 | bytes 7176193 | tf_op jit(solution)/shard_map/dot_general | solution.py:147
  366.9 0.9 maximum_select_fusion.4
  (32 shorter events, 0.2 us)
Async XLA Ops:
  7.2 1.0 copy-start
  7.2 67.7 %copy-start.5 = (s32[128,8]{0,1:T(8,128)S(1)}, s32[128,8]{0,1:T(8,128)}, u32[]{:S(2)}) copy-start(s32[128,8]{0,1:T(8,128)} %param.9) | copy-start | bytes 12292
  7.2 67.7 %copy-start.6 = (f32[128,8]{0,1:T(8,128)S(1)}, f32[128,8]{0,1:T(8,128)}, u32[]{:S(2)}) copy-start(f32[128,8]{0,1:T(8,128)} %param.10) | copy-start | bytes 12292
  7.2 141.5 %all-gather.6.cloned.1.call-start = ((), (), s32[]{:S(2)}) async-start(), calls=%async_computation.5 | async-start | bytes 4456448 | tf_op jit(solution)/shard_map/all_gather | solution.py:102
  9.0 213.9 %all-gather.8.cloned.1.call-start = ((), (), s32[]{:S(2)}) async-start(), calls=%async_computation.6 | async-start | bytes 4456448 | tf_op jit(solution)/shard_map/all_gather | solution.py:103
  67.9 91.4 %all-to-all-start.1 = ((bf16[16,128,384]{2,1,0:T(8,128)(2,1)}), bf16[16,128,384]{2,1,0:T(8,128)(2,1)S(1)}, u32[]{:S(2)}, u32[]{:S(2)}) async-start(bf16[16,128,384]{2,1,0:T(8,128)(2,1)} %param.12), calls=%async_computation.1 | async-start | bytes 3145728 | tf_op jit(solution)/shard_map/all_to_all | solution.py:98
  153.1 74.6 %collective-permute-start = (bf16[1152,1024]{1,0:T(8,128)(2,1)}, bf16[1152,1024]{1,0:T(8,128)(2,1)}, u32[]{:S(2)}, u32[]{:S(2)}) collective-permute-start(bf16[1152,1024]{1,0:T(8,128)(2,1)} %bitcast.1), channel_id=1, source_target_pairs={{0,16},{16,0},{1,17},{17,1},{2,18},{18,2},{3,19},{19,3},{4,20},{20... | collective-permute-start | bytes 7077896 | tf_op jit(solution)/shard_map/ppermute | solution.py:13
  159.3 84.0 %all-to-all-start = ((bf16[16,128,384]{2,1,0:T(8,128)(2,1)}), bf16[16,128,384]{2,1,0:T(8,128)(2,1)}, u32[]{:S(2)}, u32[]{:S(2)}) async-start(bf16[16,128,384]{2,1,0:T(8,128)(2,1)} %param.13), calls=%async_computation | async-start | bytes 3145728 | tf_op jit(solution)/shard_map/all_to_all | solution.py:98
  164.9 193.6 %reduce-scatter.2.cloned.1.call-start = ((), (), s32[]{:S(2)}) async-start(), calls=%async_computation.4 | async-start | bytes 4456448 | tf_op jit(solution)/shard_map/reduce_scatter | solution.py:143
  227.3 16.1 %collective-permute-start.1 = (bf16[1152,1024]{1,0:T(8,128)(2,1)}, bf16[1152,1024]{1,0:T(8,128)(2,1)}, u32[]{:S(2)}, u32[]{:S(2)}) collective-permute-start(bf16[1152,1024]{1,0:T(8,128)(2,1)} %bitcast.3), channel_id=1, source_target_pairs={{0,16},{16,0},{1,17},{17,1},{2,18},{18,2},{3,19},{19,3},{4,20},{20... | collective-permute-start | bytes 7077896 | tf_op jit(solution)/shard_map/ppermute | solution.py:13
  243.4 7.6 %copy-start.1 = (bf16[16,128,384]{2,1,0:T(8,128)(2,1)S(1)}, bf16[16,128,384]{2,1,0:T(8,128)(2,1)}, u32[]{:S(2)}) copy-start(bf16[16,128,384]{2,1,0:T(8,128)(2,1)} %all_to_all.12) | copy-start | bytes 4718596
  250.9 7.5 %copy-start.2 = (bf16[1152,384]{1,0:T(8,128)(2,1)}, bf16[1152,384]{1,0:T(8,128)(2,1)S(1)}, u32[]{:S(2)}) copy-start(bf16[1152,384]{1,0:T(8,128)(2,1)S(1)} %get-tuple-element.6) | copy-start | bytes 2654212
  253.9 4.6 %collective-permute-start.2 = (bf16[1152,1024]{1,0:T(8,128)(2,1)S(1)}, bf16[1152,1024]{1,0:T(8,128)(2,1)S(1)}, u32[]{:S(2)}, u32[]{:S(2)}) collective-permute-start(bf16[1152,1024]{1,0:T(8,128)(2,1)S(1)} %fusion), channel_id=1, source_target_pairs={{0,16},{16,0},{1,17},{17,1},{2,18},{18,2},{3,19},{19,3},{4,20},{20... | collective-permute-start | bytes 7077896 | tf_op jit(solution)/shard_map/ppermute | solution.py:13
  260.0 3.4 copy-start.3
  263.4 8.0 %copy-start.7 = (f32[1152,384]{1,0:T(8,128)S(1)}, f32[1152,384]{1,0:T(8,128)}, u32[]{:S(2)}) copy-start(f32[1152,384]{1,0:T(8,128)} %fusion.25) | copy-start | bytes 5308420
  263.5 8.0 %copy-start.8 = (f32[1152,384]{1,0:T(8,128)S(1)}, f32[1152,384]{1,0:T(8,128)}, u32[]{:S(2)}) copy-start(f32[1152,384]{1,0:T(8,128)} %fusion.26) | copy-start | bytes 5308420
  358.5 8.4 %copy-start.4 = (bf16[1,128,1024]{2,1,0:T(8,128)(2,1)S(1)}, bf16[1,128,1024]{2,1,0:T(8,128)(2,1)}, u32[]{:S(2)}) copy-start(bf16[1,128,1024]{2,1,0:T(8,128)(2,1)} %reduce-scatter.2.cloned.1.call-done) | copy-start | bytes 786436
  358.5 8.4 %collective-permute-start.3 = (bf16[128,1024]{1,0:T(8,128)(2,1)}, bf16[128,1024]{1,0:T(8,128)(2,1)S(1)}, u32[]{:S(2)}, u32[]{:S(2)}) collective-permute-start(bf16[128,1024]{1,0:T(8,128)(2,1)} %bitcast.43), channel_id=1, source_target_pairs={{0,16},{16,0},{1,17},{17,1},{2,18},{18,2},{3,19},{19,3},{4,20},{20... | collective-permute-start | bytes 786440 | tf_op jit(solution)/shard_map/ppermute | solution.py:13
Sparse Core Ops, SparseCore 0:
  11.3 106.5 all-gather.5
  121.3 101.5 all-gather.7
  263.6 94.8 reduce-scatter.1

commit v2 on v0

--- a/solution.py
+++ b/solution.py
@@ -1,6 +1,10 @@
+import functools
+
 import jax
 import jax.numpy as jnp
 from jax import lax
+from jax.experimental import pallas as pl
+from jax.experimental.pallas import tpu as pltpu
 from jax.sharding import PartitionSpec as P
 
 
@@ -13,7 +17,7 @@
     return lax.ppermute(part, "dp", [(0, 1), (1, 0)])
 
 
-def placed(tokens, out_grad, route_ids, route_probs, gate_store, up_store, down_store):
+def placed_sparse(tokens, out_grad, route_ids, route_probs, gate_store, up_store, down_store):
     tok_rows, model_width = tokens.shape
     top_count = route_ids.shape[1]
     experts = lax.axis_size("expert")
@@ -80,6 +84,556 @@
     grad_gate = lax.dot_general(rows_in, gate_grad, outer, preferred_element_type=f32).astype(bf16)
     grad_up = lax.dot_general(rows_in, up_grad, outer, preferred_element_type=f32).astype(bf16)
     return (grad_gate[None], grad_up[None], grad_down[None], grad_tokens)
+
+
+f32, bf16 = jnp.float32, jnp.bfloat16
+MESH = pl.DeviceIdType.MESH
+
+
+def dense_kernel(
+    experts, capacity,
+    ids_ref, probs_ref, x_ref, dy_ref, gate_ref, up_ref, down_ref,
+    grad_gate_ref, grad_up_ref, grad_down_ref, grad_tokens_ref,
+    info, info_all, gu, dn, tok, nbr_out, rows, pls, pre, act, activ, gg,
+    mine, cs_out, cs_in, comb, s_out, t_own, t_out, xr, z_out, z_in, stage, fin,
+    local_sem, info_send, info_recv, w_send, w_recv, w_own,
+    ag_up, ag_down, ag_zr, ag_xs, ag_xr, y_send, y_recv, c_send, c_recv,
+    cs_send, cs_recv, ys_send, ys_recv, xs_send, xs_recv, zs_send, zs_recv, out_sem, fin_sem,
+):
+    me, core = lax.axis_index("expert"), lax.axis_index("dp")
+    planes = experts // 4
+    z, y, x = me // 4, (me // 2) % 2, me % 2
+    x_peer, y_peer = me + 1 - 2 * x, me + 2 - 4 * y
+    tok_rows, model_width = x_ref.shape
+    width = model_width // 2
+    hid = gate_ref.shape[2]
+    pair = 2 * capacity
+    quad = 4 * capacity
+    slots = experts * capacity
+    slab = model_width // planes
+    here = pl.multiple_of(core * width, width)
+    batch0 = (((0,), (0,)), ((), ()))
+
+    def remote(src, dst, send, recv, expert=None):
+        target = {"dp": 1 - core} if expert is None else {"expert": expert}
+        return pltpu.make_async_remote_copy(
+            src_ref=src, dst_ref=dst, send_sem=send, recv_sem=recv, device_id=target, device_id_type=MESH
+        )
+
+    def at(start, size):
+        return pl.ds(pl.multiple_of(start, size), size)
+
+    def peer_of(k):
+        return lax.rem(me + k, experts)
+
+    barrier = pltpu.get_barrier_semaphore()
+
+    def greet(k, carry):
+        pl.semaphore_signal(barrier, inc=1, device_id={"expert": peer_of(k)}, device_id_type=MESH)
+        return carry
+
+    lax.fori_loop(1, experts, greet, 0)
+    pl.semaphore_signal(barrier, inc=1, device_id={"dp": 1 - core}, device_id_type=MESH)
+
+    own_copies = []
+    for a, ref in enumerate((x_ref, dy_ref)):
+        own_copies.append(
+            pltpu.make_async_copy(ref.at[:, pl.ds(here, width)], tok.at[a, z, at(x * tok_rows, tok_rows), :], local_sem.at[a])
+        )
+    own_rows = at((me % 4) * tok_rows, tok_rows)
+    own_panels = [
+        pltpu.make_async_copy(gate_ref.at[me], gu.at[z, own_rows, pl.ds(0, hid)], w_own.at[0]),
+        pltpu.make_async_copy(up_ref.at[me], gu.at[z, own_rows, pl.ds(hid, hid)], w_own.at[1]),
+        pltpu.make_async_copy(down_ref.at[me], dn.at[z, own_rows, :], w_own.at[2]),
+    ]
+    for copy in own_copies:
+        copy.start()
+    for copy in own_panels:
+        copy.start()
+    pl.semaphore_wait(barrier, experts)
+
+    def w_copy(w, target, owner):
+        spot = at((owner % 4) * tok_rows, tok_rows)
+        if w == 0:
+            src, dst = gate_ref, gu.at[owner // 4, spot, pl.ds(0, hid)]
+        elif w == 1:
+            src, dst = up_ref, gu.at[owner // 4, spot, pl.ds(hid, hid)]
+        else:
+            src, dst = down_ref, dn.at[owner // 4, spot, :]
+        return remote(src.at[target], dst, w_send.at[w, target], w_recv.at[w, owner], target)
+
+    def start_panel(w, first, last):
+        def body(k, carry):
+            w_copy(w, peer_of(k), me).start()
+            return carry
+
+        lax.fori_loop(first, last, body, 0)
+
+    def wait_panel(w, source):
+        w_copy(w, source, source).wait_recv()
+
+    def tok_block(a, zs, xs):
+        return tok.at[a, zs, at(xs * tok_rows, tok_rows), :]
+
+    def ag_copy(a, zs, direction):
+        block = tok_block(a, zs, x)
+        if direction == 0:
+            return remote(block, block, ag_up.at[a, zs], ag_zr.at[a, zs], me + 4)
+        if direction == 1:
+            return remote(block, block, ag_down.at[a, zs], ag_zr.at[a, zs], me - 4)
+        return remote(block, block, ag_xs.at[a, zs], ag_xr.at[a, zs], x_peer)
+
+    def walk(t):
+        return z + ((t + 1) // 2) * (1 - 2 * (t % 2))
+
+    def inside(zs):
+        return jnp.logical_and(zs >= 0, zs < planes)
+
+    def forwards(zs):
+        return (
+            jnp.logical_and(zs <= z, z < planes - 1),
+            jnp.logical_and(zs >= z, z > 0),
+        )
+
+    def send_block(a, zs):
+        go_up, go_down = forwards(zs)
+
+        @pl.when(go_up)
+        def _():
+            ag_copy(a, zs, 0).start()
+
+        @pl.when(go_down)
+        def _():
+            ag_copy(a, zs, 1).start()
+
+        ag_copy(a, zs, 2).start()
+
+    for a in range(2):
+        own_copies[a].wait()
+        send_block(a, z)
+    start_panel(0, 1, experts)
+
+    ids, probs = ids_ref[...], probs_ref[...]
+    named_by = lax.broadcasted_iota(jnp.int32, (experts,) + ids.shape, 0) == ids[None, :, :]
+    weight = jnp.sum(jnp.where(named_by, probs[None, :, :], 0.0), axis=1)
+    named = jnp.sum(jnp.where(named_by, 1.0, 0.0), axis=1)
+    before = lax.broadcasted_iota(jnp.int32, (tok_rows, tok_rows), 0) < lax.broadcasted_iota(
+        jnp.int32, (tok_rows, tok_rows), 1
+    )
+    rank = jnp.dot(named.astype(bf16), jnp.where(before, 1.0, 0.0).astype(bf16), preferred_element_type=f32)
+    rank = jnp.where(named > 0.5, rank + (x * capacity).astype(f32), -1.0)
+    line = lax.broadcasted_iota(jnp.int32, (experts, 8, tok_rows), 1)
+    info[...] = jnp.where(line == 0, rank[:, None, :], weight[:, None, :])
+    info_all[me] = info[at(z * 4, 4)]
+
+    def info_copy(target, owner):
+        return remote(
+            info.at[at((target // 4) * 4, 4)], info_all.at[owner], info_send.at[target], info_recv.at[owner], target
+        )
+
+    def send_info(k, carry):
+        info_copy(peer_of(k), me).start()
+        return carry
+
+    lax.fori_loop(1, experts, send_info, 0)
+
+    hops = 2 * planes - 2
+    for t in range(1, hops + 1):
+        zs = walk(t)
+
+        @pl.when(inside(zs))
+        def _():
+            for a in range(2):
+                remote(tok_block(a, zs, x), tok_block(a, zs, x), ag_up.at[a, zs], ag_zr.at[a, zs], x_peer).wait_recv()
+                send_block(a, zs)
+
+        start_panel(1, 1 + (t - 1) * (experts - 1) // hops, 1 + t * (experts - 1) // hops)
+
+    def wait_info(k, carry):
+        source = peer_of(k)
+        info_copy(source, source).wait_recv()
+        return carry
+
+    lax.fori_loop(1, experts, wait_info, 0)
+
+    def pair_rows(zs, ys):
+        return at((2 * zs + ys) * pair, pair)
+
+    def places(zs, expert_index):
+        first = 4 * zs + 2 * y
+        both = jnp.concatenate(
+            [info_all[first, expert_index, :, :], info_all[first + 1, expert_index, :, :]], axis=1
+        )
+        hit = both[0:1, :] == lax.broadcasted_iota(jnp.int32, (pair, 2 * tok_rows), 0).astype(f32)
+        prob = jnp.sum(jnp.where(hit, both[1:2, :], 0.0), axis=1, keepdims=True)
+        return jnp.where(hit, 1.0, 0.0).astype(bf16), prob
+
+    def y_copy(a, zs, ys):
+        return remote(
+            nbr_out.at[a, zs], rows.at[a, core, pair_rows(zs, ys), :], y_send.at[a, zs], y_recv.at[a, zs], y_peer
+        )
+
+    def core_copy(a, half, zs, ys):
+        block = rows.at[a, half, pair_rows(zs, ys), :]
+        return remote(block, block, c_send.at[a, 2 * zs + ys], c_recv.at[a, 2 * zs + ys])
+
+    mine_q = me % 4
+    peer_q = y_peer % 4
+
+    def gather(t, carry):
+        zs = walk(t)
+
+        @pl.when(inside(zs))
+        def _():
+            own_place, own_prob = places(zs, mine_q)
+            nbr_place, nbr_prob = places(zs, peer_q)
+            pls[zs, pl.ds(0, pair), :] = own_place
+            pls[zs, pl.ds(pair, pair), :] = nbr_place
+            for a in range(2):
+                ag_copy(a, zs, 2).wait_recv()
+                got = jnp.dot(own_place, tok[a, zs], preferred_element_type=f32)
+                lent = jnp.dot(nbr_place, tok[a, zs], preferred_element_type=f32)
+                if a == 1:
+                    got, lent = got * own_prob, lent * nbr_prob
+                nbr_out[a, zs] = lent.astype(bf16)
+                y_copy(a, zs, y).start()
+                rows[a, core, pair_rows(zs, y), :] = got.astype(bf16)
+                core_copy(a, core, zs, y).start()
+
+        def more(k, inner):
+            @pl.when(k < experts)
+            def _():
+                w_copy(2, peer_of(k), me).start()
+
+            return inner
+
+        lax.fori_loop(1 + 3 * t, 4 + 3 * t, more, 0)
+        return carry
+
+    lax.fori_loop(0, hops + 1, gather, 0)
+
+    def pass_on(t, carry):
+        zs = walk(t)
+
+        @pl.when(inside(zs))
+        def _():
+            for a in range(2):
+                y_copy(a, zs, 1 - y).wait_recv()
+                core_copy(a, core, zs, 1 - y).start()
+
+        return carry
+
+    lax.fori_loop(0, hops + 1, pass_on, 0)
+
+    def wait_core(p, carry):
+        for a in range(2):
+            core_copy(a, 1 - core, p // 2, p % 2).wait_recv()
+        return carry
+
+    lax.fori_loop(0, 2 * planes, wait_core, 0)
+    for w in range(2):
+        own_panels[w].wait()
+
+        def wait_gu(k, carry):
+            wait_panel(w, peer_of(k))
+            return carry
+
+        lax.fori_loop(1, experts, wait_gu, 0)
+
+    def slab_of(a, g, spot):
+        half, off = (g * slab) // width, (g * slab) % width
+        return rows[a, half, spot, pl.ds(off, slab)]
+
+    def forward(m, carry):
+        spot = at(m * quad, quad)
+        total = jnp.dot(slab_of(0, 0, spot), gu[0], preferred_element_type=f32)
+        for g in range(1, planes):
+            total += jnp.dot(slab_of(0, g, spot), gu[g], preferred_element_type=f32)
+        pre[spot, :] = total
+        return carry
+
+    lax.fori_loop(0, planes, forward, 0)
+    own_panels[2].wait()
+    for g in range(planes):
+        for q in range(4):
+            source = 4 * g + q
+
+            @pl.when(source != me)
+            def _():
+                wait_panel(2, source)
+
+        def backward(m, carry):
+            spot = at(m * quad, quad)
+            part = jnp.dot(slab_of(1, g, spot), dn[g], preferred_element_type=f32)
+            if g == 0:
+                act[spot, :] = part
+            else:
+                act[spot, :] += part
+            return carry
+
+        lax.fori_loop(0, planes, backward, 0)
+
+    def pointwise(m, carry):
+        spot = at(m * 16, 16)
+        gate_pre, up_pre, act_grad = pre[spot, pl.ds(0, hid)], pre[spot, pl.ds(hid, hid)], act[spot, :]
+        sig = jax.nn.sigmoid(gate_pre)
+        activ[spot, :] = (gate_pre * sig * up_pre).astype(bf16)
+        gg[spot, pl.ds(0, hid)] = (act_grad * up_pre * sig * (1.0 + gate_pre * (1.0 - sig))).astype(bf16)
+        gg[spot, pl.ds(hid, hid)] = (act_grad * gate_pre * sig).astype(bf16)
+        return carry
+
+    back = (((1,), (1,)), ((), ()))
+    half_planes = planes // 2
+
+    def cs_copy(d):
+        return remote(cs_out.at[d], cs_in.at[d], cs_send.at[d], cs_recv.at[d])
+
+    def ys_copy(d):
+        return remote(s_out.at[d], comb.at[d, pl.ds(pair, pair), :], ys_send.at[d], ys_recv.at[d], y_peer)
+
+    def xs_copy(d):
+        return remote(t_out.at[d], xr.at[d], xs_send.at[d], xs_recv.at[d], x_peer)
+
+    def slot_step(d):
+        lax.fori_loop(d * (quad // 16), (d + 1) * (quad // 16), pointwise, 0)
+        spot = pl.ds(d * quad, quad)
+        for i in range(half_planes):
+            there = (1 - core) * half_planes + i
+            cs_out[d, :, pl.ds(i * slab, slab)] = lax.dot_general(
+                gg[spot, :], gu[there], back, preferred_element_type=f32
+            ).astype(bf16)
+        cs_copy(d).start()
+        for i in range(half_planes):
+            mine[d, :, pl.ds(i * slab, slab)] = lax.dot_general(
+                gg[spot, :], gu[core * half_planes + i], back, preferred_element_type=f32
+            )
+
+    def slot_sum(d):
+        cs_copy(d).wait_recv()
+        away, home = at((1 - y) * pair, pair), at(y * pair, pair)
+        s_out[d] = (mine[d, away, :] + cs_in[d, away, :].astype(f32)).astype(bf16)
+        ys_copy(d).start()
+        comb[d, pl.ds(0, pair), :] = (mine[d, home, :] + cs_in[d, home, :].astype(f32)).astype(bf16)
+
+    def token_step(d):
+        ys_copy(d).wait_recv()
+        t_out[d] = lax.dot_general(
+            pls[d, :, at((1 - x) * tok_rows, tok_rows)], comb[d], batch0, preferred_element_type=f32
+        ).astype(bf16)
+        xs_copy(d).start()
+        t_own[d] = lax.dot_general(
+            pls[d, :, at(x * tok_rows, tok_rows)], comb[d], batch0, preferred_element_type=f32
+        )
+
+    def z_copy(d, up):
+        if up:
+            return remote(z_out.at[d], z_in.at[0, d], zs_send.at[d], zs_recv.at[0, d], me + 4)
+        return remote(z_out.at[d], z_in.at[1, d], zs_send.at[d], zs_recv.at[1, d], me - 4)
+
+    def z_take(d, side):
+        remote(z_out.at[d], z_in.at[side, d], zs_send.at[d], zs_recv.at[side, d], x_peer).wait_recv()
+        t_own[d] += z_in[side, d].astype(f32)
+
+    def z_step(d):
+        xs_copy(d).wait_recv()
+        t_own[d] += xr[d].astype(f32)
+
+        @pl.when(jnp.logical_and(d > z, z > 0))
+        def _():
+            z_take(d, 0)
+
+        @pl.when(jnp.logical_and(d < z, z < planes - 1))
+        def _():
+            z_take(d, 1)
+
+        @pl.when(d > z)
+        def _():
+            z_out[d] = t_own[d].astype(bf16)
+            z_copy(d, True).start()
+
+        @pl.when(d < z)
+        def _():
+            z_out[d] = t_own[d].astype(bf16)
+            z_copy(d, False).start()
+
+    tile = width // 4
+
+    def out_copy(w, i):
+        span = at(i * tile, tile)
+        return pltpu.make_async_copy(
+            stage.at[w, span, :], (grad_gate_ref, grad_up_ref, grad_down_ref)[w].at[span, :], out_sem.at[w, i]
+        )
+
+    def weight_grads(first, last):
+        def body(i, carry):
+            half, off, span = i // 4, at((i % 4) * tile, tile), at(i * tile, tile)
+            both = lax.dot_general(rows[0, half, :, off], gg[...], batch0, preferred_element_type=f32)
+            stage[0, span, :] = both[:, :hid].astype(bf16)
+            stage[1, span, :] = both[:, hid:].astype(bf16)
+            stage[2, span, :] = lax.dot_general(
+                rows[1, half, :, off], activ[...], batch0, preferred_element_type=f32
+            ).astype(bf16)
+            for w in range(3):
+                out_copy(w, i).start()
+            return carry
+
+        lax.fori_loop(first, last, body, 0)
+
+    order = []
+    for i in range(half_planes):
+        order += [i, planes - 1 - i]
+    for i, d in enumerate(order):
+        slot_step(d)
+        if i > 0:
+            slot_sum(order[i - 1])
+    slot_sum(order[-1])
+    weight_grads(0, 3)
+    token_step(order[0])
+    weight_grads(3, 6)
+    for i in range(1, planes):
+        token_step(order[i])
+        d = order[i - 1]
+
+        @pl.when(d != z)
+        def _():
+            z_step(d)
+
+        if i == 1:
+            weight_grads(6, 8)
+
+    @pl.when(order[-1] != z)
+    def _():
+        z_step(order[-1])
+
+    xs_copy(z).wait_recv()
+    t_own[z] += xr[z].astype(f32)
+
+    @pl.when(z > 0)
+    def _():
+        z_take(z, 0)
+
+    @pl.when(z < planes - 1)
+    def _():
+        z_take(z, 1)
+
+    fin[...] = t_own[z].astype(bf16)
+    home_spot = grad_tokens_ref.at[:, pl.ds(here, width)]
+    last = remote(fin, home_spot, fin_sem.at[0], fin_sem.at[1])
+    last.start()
+    keep = pltpu.make_async_copy(fin, home_spot, fin_sem.at[2])
+    keep.start()
+
+    def drain_peers(k, carry):
+        target = peer_of(k)
+        for w in range(3):
+            w_copy(w, target, me).wait_send()
+        info_copy(target, me).wait_send()
+        return carry
+
+    lax.fori_loop(1, experts, drain_peers, 0)
+
+    def drain_tokens(zs, carry):
+        go_up, go_down = forwards(zs)
+        for a in range(2):
+
+            @pl.when(go_up)
+            def _():
+                ag_copy(a, zs, 0).wait_send()
+
+            @pl.when(go_down)
+            def _():
+                ag_copy(a, zs, 1).wait_send()
+
+            ag_copy(a, zs, 2).wait_send()
+            y_copy(a, zs, y).wait_send()
+            for ys in range(2):
+                core_copy(a, core, zs, ys).wait_send()
+        cs_copy(zs).wait_send()
+        ys_copy(zs).wait_send()
+        xs_copy(zs).wait_send()
+
+        @pl.when(zs > z)
+        def _():
+            z_copy(zs, True).wait_send()
+
+        @pl.when(zs < z)
+        def _():
+            z_copy(zs, False).wait_send()
+
+        return carry
+
+    lax.fori_loop(0, planes, drain_tokens, 0)
+
+    def drain_out(i, carry):
+        for w in range(3):
+            out_copy(w, i).wait()
+        return carry
+
+    lax.fori_loop(0, 8, drain_out, 0)
+    keep.wait()
+    last.wait()
+
+
+def placed_dense(tokens, out_grad, route_ids, route_probs, gate_store, up_store, down_store):
+    tok_rows, model_width = tokens.shape
+    top_count = route_ids.shape[1]
+    experts, _, hid = gate_store.shape
+    capacity = 9 * tok_rows * top_count // (8 * experts)
+    slots, width, planes = experts * capacity, model_width // 2, experts // 4
+    pair, quad, slab = 2 * capacity, 4 * capacity, model_width // planes
+    vmem, dma = pltpu.VMEM, pltpu.SemaphoreType.DMA
+    anywhere, on_chip = pl.BlockSpec(memory_space=pl.ANY), pl.BlockSpec(memory_space=pltpu.VMEM)
+    scratch = [
+        vmem((experts, 8, tok_rows), f32),
+        vmem((experts, 4, 8, tok_rows), f32),
+        vmem((planes, slab, 2 * hid), bf16),
+        vmem((planes, slab, hid), bf16),
+        vmem((2, planes, 2 * tok_rows, width), bf16),
+        vmem((2, planes, pair, width), bf16),
+        vmem((2, 2, slots, width), bf16),
+        vmem((planes, quad, 2 * tok_rows), bf16),
+        vmem((slots, 2 * hid), f32),
+        vmem((slots, hid), f32),
+        vmem((slots, hid), bf16),
+        vmem((slots, 2 * hid), bf16),
+        vmem((planes, quad, width), f32),
+        vmem((planes, quad, width), bf16),
+        vmem((planes, quad, width), bf16),
+        vmem((planes, quad, width), bf16),
+        vmem((planes, pair, width), bf16),
+        vmem((planes, tok_rows, width), f32),
+        vmem((planes, tok_rows, width), bf16),
+        vmem((planes, tok_rows, width), bf16),
+        vmem((planes, tok_rows, width), bf16),
+        vmem((2, planes, tok_rows, width), bf16),
+        vmem((3, model_width, hid), bf16),
+        vmem((tok_rows, width), bf16),
+        dma((2,)), dma((experts,)), dma((experts,)), dma((3, experts)), dma((3, experts)), dma((3,)),
+        dma((2, planes)), dma((2, planes)), dma((2, planes)), dma((2, planes)), dma((2, planes)),
+        dma((2, planes)), dma((2, planes)), dma((2, 2 * planes)), dma((2, 2 * planes)),
+        dma((planes,)), dma((planes,)), dma((planes,)), dma((planes,)),
+        dma((planes,)), dma((planes,)), dma((planes,)), dma((2, planes)), dma((3, 8)), dma((3,)),
+    ]
+    grad = jax.ShapeDtypeStruct((model_width, hid), bf16)
+    outs = pl.pallas_call(
+        functools.partial(dense_kernel, experts, capacity),
+        out_shape=(grad, grad, grad, jax.ShapeDtypeStruct((tok_rows, model_width), bf16)),
+        in_specs=[on_chip, on_chip] + [anywhere] * 5,
+        out_specs=(anywhere,) * 4,
+        scratch_shapes=scratch,
+        compiler_params=pltpu.CompilerParams(
+            collective_id=0, has_side_effects=True, vmem_limit_bytes=60 * 1024 * 1024
+        ),
+    )(route_ids.T, route_probs.T, tokens, out_grad, gate_store, up_store, down_store)
+    return (outs[0][None], outs[1][None], outs[2][None], outs[3])
+
+
+def placed(tokens, out_grad, route_ids, route_probs, gate_store, up_store, down_store):
+    experts, top_count = lax.axis_size("expert"), route_ids.shape[1]
+    capacity = 9 * tokens.shape[0] * top_count // (8 * experts)
+    dense = 4 * top_count >= experts and experts % 8 == 0 and capacity % 8 == 0
+    body = placed_dense if dense else placed_sparse
+    return body(tokens, out_grad, route_ids, route_probs, gate_store, up_store, down_store)
 
 
 def solution(mesh):

time: 330 us -> 253 us (0.77)
  Pallas kernels: 0 us -> 245 us
  waiting for transfers between devices: 184 us -> 0 us
  matrix products: 59.6 us -> 0 us
  starting transfers between devices: 40.7 us -> 0 us
  blocking collectives: 40.6 us -> 0 us
  local copies, waits for them, and re-layouts: 0.23 us -> 6.99 us
    pallas_call x0 -> x1, Pallas kernels: none -> 245 us  [placed_dense(): pl.pallas_call(functools.partial(dense_kernel, experts, capacity), out_sh...]
    all_to_all x5 -> x0, waiting for transfers between devices: 181 us -> none  [the longest x3 133 us: exchange(): return lax.all_to_all(a, 'expert', split_axis=0, concat_axis=0, tiled=True)]
    dot_general x14 -> x0, matrix products: 59.6 us -> none  [the longest x1 8.14 us: placed(): lax.dot_general(rows_in, up_grad, outer, preferred_element_type=f32)]
    all_to_all x1 -> x0, blocking collectives: 40.6 us -> none  [panel(): lax.all_to_all(store, 'expert', split_axis=0, concat_axis=1, tiled=True)[0]]
    all_to_all x5 -> x0, starting transfers between devices: 33.5 us -> none  [the longest x3 19.9 us: exchange(): return lax.all_to_all(a, 'expert', split_axis=0, concat_axis=0, tiled=True)]
    ppermute x4 -> x0, starting transfers between devices: 7.27 us -> none  [swapped(): return lax.ppermute(part, 'dp', [(0, 1), (1, 0)])]
    unnamed x20 -> x10, local copies, waits for them, and re-layouts: 0.05 us -> 6.99 us
  transfers between devices with their start and end apart: 9 -> 0, of which waited for: 6 -> 0; matrix products, arithmetic and copies ran while one was open for 14% -> 0% of each run, Pallas kernels for 0% -> 0%
where the time goes in v2:
time: 253 us
  Pallas kernels  245 us (97%)
  local copies, waits for them, and re-layouts  6.99 us (3%)
    pallas_call x1, Pallas kernels, placed_dense(): pl.pallas_call(functools.partial(dense_kernel, experts, capacity), out_sh...  245 us
    unnamed x10, local copies, waits for them, and re-layouts  6.99 us

profile of v2, /device:TPU:21, one launch (start us, length us, event | category | flops | bytes accessed | tf_op | source)
XLA Modules:
  0.0 252.6 jit_solution(13275712994650486641)
XLA Ops:
  0.6 244.9 %shard_map.102 = (bf16[2048,384]{1,0:T(8,128)(2,1)}, bf16[2048,384]{1,0:T(8,128)(2,1)}, bf16[2048,384]{1,0:T(8,128)(2,1)}, bf16[128,2048]{1,0:T(8,128)(2,1)}) custom-call(s32[8,128]{1,0:T(8,128)} %bitcast.8, f32[8,128]{1,0:T(8,128)} %bitcast.9, bf16[128,2048]{1,0:T(8,128)(2,1)} %x_ref.1, bf16[128,2048]{1,0:T(8,128)(2,1)} %dy_ref.1, ...), custom_call_target="tpu_custom_call" | custom-call | tf_op jit(solution)/shard_map/pallas_call | solution.py:618
  245.5 0.0 copy-start.1
  245.6 2.8 %copy.15 = bf16[1,2048,384]{2,1,0:T(8,128)(2,1)} copy(bf16[1,2048,384]{2,1,0:T(8,128)(2,1)} %bitcast.7) | data formatting | bytes 3145728
  248.4 0.0 copy-done.1
  248.4 0.0 copy-start
  248.4 1.1 copy.16
  249.5 0.8 copy-done
  250.4 0.0 copy-start.2
  250.4 1.1 copy.17
  251.5 0.3 copy-done.2
  251.8 0.8 copy.18
Async XLA Ops:
  245.5 2.8 %copy-start.1 = (bf16[2048,384]{1,0:T(8,128)(2,1)S(1)}, bf16[2048,384]{1,0:T(8,128)(2,1)}, u32[]{:S(2)}) copy-start(bf16[2048,384]{1,0:T(8,128)(2,1)} %get-tuple-element.9) | copy-start | bytes 4718596
  248.4 2.0 copy-start
  250.4 1.4 copy-start.2

commit v3 on v2

--- a/solution.py
+++ b/solution.py
@@ -211,7 +211,6 @@
     for a in range(2):
         own_copies[a].wait()
         send_block(a, z)
-    start_panel(0, 1, experts)
 
     ids, probs = ids_ref[...], probs_ref[...]
     named_by = lax.broadcasted_iota(jnp.int32, (experts,) + ids.shape, 0) == ids[None, :, :]
@@ -236,18 +235,7 @@
         return carry
 
     lax.fori_loop(1, experts, send_info, 0)
-
-    hops = 2 * planes - 2
-    for t in range(1, hops + 1):
-        zs = walk(t)
-
-        @pl.when(inside(zs))
-        def _():
-            for a in range(2):
-                remote(tok_block(a, zs, x), tok_block(a, zs, x), ag_up.at[a, zs], ag_zr.at[a, zs], x_peer).wait_recv()
-                send_block(a, zs)
-
-        start_panel(1, 1 + (t - 1) * (experts - 1) // hops, 1 + t * (experts - 1) // hops)
+    start_panel(0, 1, experts)
 
     def wait_info(k, carry):
         source = peer_of(k)
@@ -280,37 +268,49 @@
     mine_q = me % 4
     peer_q = y_peer % 4
 
-    def gather(t, carry):
-        zs = walk(t)
-
-        @pl.when(inside(zs))
-        def _():
-            own_place, own_prob = places(zs, mine_q)
-            nbr_place, nbr_prob = places(zs, peer_q)
-            pls[zs, pl.ds(0, pair), :] = own_place
-            pls[zs, pl.ds(pair, pair), :] = nbr_place
+    def gather(zs):
+        own_place, own_prob = places(zs, mine_q)
+        nbr_place, nbr_prob = places(zs, peer_q)
+        pls[zs, pl.ds(0, pair), :] = own_place
+        pls[zs, pl.ds(pair, pair), :] = nbr_place
+        for a in range(2):
+            ag_copy(a, zs, 2).wait_recv()
+            got = jnp.dot(own_place, tok[a, zs], preferred_element_type=f32)
+            lent = jnp.dot(nbr_place, tok[a, zs], preferred_element_type=f32)
+            if a == 1:
+                got, lent = got * own_prob, lent * nbr_prob
+            nbr_out[a, zs] = lent.astype(bf16)
+            y_copy(a, zs, y).start()
+            rows[a, core, pair_rows(zs, y), :] = got.astype(bf16)
+            core_copy(a, core, zs, y).start()
+
+    hops = 2 * planes - 2
+    others = experts - 1
+
+    def spread(t, carry):
+        zs, ready = walk(t), walk(t - 1)
+
+        @pl.when(jnp.logical_and(t <= hops, inside(zs)))
+        def _():
             for a in range(2):
-                ag_copy(a, zs, 2).wait_recv()
-                got = jnp.dot(own_place, tok[a, zs], preferred_element_type=f32)
-                lent = jnp.dot(nbr_place, tok[a, zs], preferred_element_type=f32)
-                if a == 1:
-                    got, lent = got * own_prob, lent * nbr_prob
-                nbr_out[a, zs] = lent.astype(bf16)
-                y_copy(a, zs, y).start()
-                rows[a, core, pair_rows(zs, y), :] = got.astype(bf16)
-                core_copy(a, core, zs, y).start()
-
-        def more(k, inner):
-            @pl.when(k < experts)
-            def _():
-                w_copy(2, peer_of(k), me).start()
-
-            return inner
-
-        lax.fori_loop(1 + 3 * t, 4 + 3 * t, more, 0)
-        return carry
-
-    lax.fori_loop(0, hops + 1, gather, 0)
+                remote(tok_block(a, zs, x), tok_block(a, zs, x), ag_up.at[a, zs], ag_zr.at[a, zs], x_peer).wait_recv()
+                send_block(a, zs)
+
+        @pl.when(t < planes)
+        def _():
+            start_panel(1, 1 + (t - 1) * others // (planes - 1), 1 + t * others // (planes - 1))
+
+        @pl.when(t >= planes)
+        def _():
+            start_panel(2, 1 + (t - planes) * others // planes, 1 + (t - planes + 1) * others // planes)
+
+        @pl.when(inside(ready))
+        def _():
+            gather(ready)
+
+        return carry
+
+    lax.fori_loop(1, hops + 2, spread, 0)
 
     def pass_on(t, carry):
         zs = walk(t)

time: 253 us -> 209 us (0.83)
  Pallas kernels: 245 us -> 200 us
    pallas_call x1, Pallas kernels: 245 us -> 200 us  [placed_dense(): pl.pallas_call(functools.partial(dense_kernel, experts, capacity), out_sh...]
where the time goes in v3:
time: 209 us; the launch traced here: 208 us
  Pallas kernels  200 us (96%)
  local copies, waits for them, and re-layouts  6.99 us (3%)
    pallas_call x1, Pallas kernels, placed_dense(): pl.pallas_call(functools.partial(dense_kernel, experts, capacity), out_sh...  200 us
    unnamed x10, local copies, waits for them, and re-layouts  6.99 us

profile of v3, /device:TPU:21, one launch (start us, length us, event | category | flops | bytes accessed | tf_op | source)
XLA Modules:
  0.0 207.8 jit_solution(6319965396999356263)
XLA Ops:
  0.6 200.1 %shard_map.102 = (bf16[2048,384]{1,0:T(8,128)(2,1)}, bf16[2048,384]{1,0:T(8,128)(2,1)}, bf16[2048,384]{1,0:T(8,128)(2,1)}, bf16[128,2048]{1,0:T(8,128)(2,1)}) custom-call(s32[8,128]{1,0:T(8,128)} %bitcast.8, f32[8,128]{1,0:T(8,128)} %bitcast.9, bf16[128,2048]{1,0:T(8,128)(2,1)} %x_ref.1, bf16[128,2048]{1,0:T(8,128)(2,1)} %dy_ref.1, ...), custom_call_target="tpu_custom_call" | custom-call | tf_op jit(solution)/shard_map/pallas_call | solution.py:618
  200.8 0.0 copy-start.1
  200.8 2.8 %copy.15 = bf16[1,2048,384]{2,1,0:T(8,128)(2,1)} copy(bf16[1,2048,384]{2,1,0:T(8,128)(2,1)} %bitcast.7) | data formatting | bytes 3145728
  203.6 0.0 copy-done.1
  203.6 0.0 copy-start
  203.6 1.1 copy.16
  204.8 0.8 copy-done
  205.6 0.0 copy-start.2
  205.6 1.1 copy.17
  206.7 0.3 copy-done.2
  207.0 0.8 copy.18
Async XLA Ops:
  200.8 2.8 %copy-start.1 = (bf16[2048,384]{1,0:T(8,128)(2,1)S(1)}, bf16[2048,384]{1,0:T(8,128)(2,1)}, u32[]{:S(2)}) copy-start(bf16[2048,384]{1,0:T(8,128)(2,1)} %get-tuple-element.9) | copy-start | bytes 4718596
  203.6 2.0 copy-start
  205.6 1.4 copy-start.2

commit v4 on v3

--- a/solution.py
+++ b/solution.py
@@ -88,6 +88,8 @@
 
 f32, bf16 = jnp.float32, jnp.bfloat16
 MESH = pl.DeviceIdType.MESH
+CUTS = 2
+Y_LAG, X_LAG, HOP_LAG = 6, 2, 2
 
 
 def dense_kernel(
@@ -98,7 +100,7 @@
     mine, cs_out, cs_in, comb, s_out, t_own, t_out, xr, z_out, z_in, stage, fin,
     local_sem, info_send, info_recv, w_send, w_recv, w_own,
     ag_up, ag_down, ag_zr, ag_xs, ag_xr, y_send, y_recv, c_send, c_recv,
-    cs_send, cs_recv, ys_send, ys_recv, xs_send, xs_recv, zs_send, zs_recv, out_sem, fin_sem,
+    cs_send, cs_recv, ys_send, ys_recv, xs_send, xs_recv, zs_send, zs_recv, out_sem, fin_send, fin_recv, fin_keep,
 ):
     me, core = lax.axis_index("expert"), lax.axis_index("dp")
     planes = experts // 4
@@ -268,21 +270,23 @@
     mine_q = me % 4
     peer_q = y_peer % 4
 
-    def gather(zs):
+    def gather(a, zs):
         own_place, own_prob = places(zs, mine_q)
         nbr_place, nbr_prob = places(zs, peer_q)
-        pls[zs, pl.ds(0, pair), :] = own_place
-        pls[zs, pl.ds(pair, pair), :] = nbr_place
-        for a in range(2):
-            ag_copy(a, zs, 2).wait_recv()
-            got = jnp.dot(own_place, tok[a, zs], preferred_element_type=f32)
-            lent = jnp.dot(nbr_place, tok[a, zs], preferred_element_type=f32)
-            if a == 1:
-                got, lent = got * own_prob, lent * nbr_prob
-            nbr_out[a, zs] = lent.astype(bf16)
-            y_copy(a, zs, y).start()
-            rows[a, core, pair_rows(zs, y), :] = got.astype(bf16)
-            core_copy(a, core, zs, y).start()
+        if a == 0:
+            pls[zs, pl.ds(0, pair), :] = own_place
+            pls[zs, pl.ds(pair, pair), :] = nbr_place
+        ag_copy(a, zs, 2).wait_recv()
+        lent = jnp.dot(nbr_place, tok[a, zs], preferred_element_type=f32)
+        if a == 1:
+            lent = lent * nbr_prob
+        nbr_out[a, zs] = lent.astype(bf16)
+        y_copy(a, zs, y).start()
+        got = jnp.dot(own_place, tok[a, zs], preferred_element_type=f32)
+        if a == 1:
+            got = got * own_prob
+        rows[a, core, pair_rows(zs, y), :] = got.astype(bf16)
+        core_copy(a, core, zs, y).start()
 
     hops = 2 * planes - 2
     others = experts - 1
@@ -293,7 +297,8 @@
         @pl.when(jnp.logical_and(t <= hops, inside(zs)))
         def _():
             for a in range(2):
-                remote(tok_block(a, zs, x), tok_block(a, zs, x), ag_up.at[a, zs], ag_zr.at[a, zs], x_peer).wait_recv()
+                block = tok_block(a, zs, x)
+                remote(block, block, ag_up.at[a, zs], ag_zr.at[a, zs], x_peer).wait_recv()
                 send_block(a, zs)
 
         @pl.when(t < planes)
@@ -306,31 +311,32 @@
 
         @pl.when(inside(ready))
         def _():
-            gather(ready)
-
-        return carry
-
-    lax.fori_loop(1, hops + 2, spread, 0)
-
-    def pass_on(t, carry):
-        zs = walk(t)
-
-        @pl.when(inside(zs))
-        def _():
             for a in range(2):
+                gather(a, ready)
+
+        return carry
+
+    def collect(a):
+        def pass_on(t, carry):
+            zs = walk(t)
+
+            @pl.when(inside(zs))
+            def _():
                 y_copy(a, zs, 1 - y).wait_recv()
                 core_copy(a, core, zs, 1 - y).start()
 
-        return carry
-
-    lax.fori_loop(0, hops + 1, pass_on, 0)
-
-    def wait_core(p, carry):
-        for a in range(2):
+            return carry
+
+        lax.fori_loop(0, hops + 1, pass_on, 0)
+
+        def wait_core(p, carry):
             core_copy(a, 1 - core, p // 2, p % 2).wait_recv()
-        return carry
-
-    lax.fori_loop(0, 2 * planes, wait_core, 0)
+            return carry
+
+        lax.fori_loop(0, 2 * planes, wait_core, 0)
+
+    lax.fori_loop(1, hops + 2, spread, 0)
+    collect(0)
     for w in range(2):
         own_panels[w].wait()
 
@@ -353,6 +359,7 @@
         return carry
 
     lax.fori_loop(0, planes, forward, 0)
+    collect(1)
     own_panels[2].wait()
     for g in range(planes):
         for q in range(4):
@@ -383,78 +390,110 @@
         return carry
 
     back = (((1,), (1,)), ((), ()))
-    half_planes = planes // 2
-
-    def cs_copy(d):
-        return remote(cs_out.at[d], cs_in.at[d], cs_send.at[d], cs_recv.at[d])
-
-    def ys_copy(d):
-        return remote(s_out.at[d], comb.at[d, pl.ds(pair, pair), :], ys_send.at[d], ys_recv.at[d], y_peer)
-
-    def xs_copy(d):
-        return remote(t_out.at[d], xr.at[d], xs_send.at[d], xs_recv.at[d], x_peer)
-
-    def slot_step(d):
-        lax.fori_loop(d * (quad // 16), (d + 1) * (quad // 16), pointwise, 0)
-        spot = pl.ds(d * quad, quad)
-        for i in range(half_planes):
-            there = (1 - core) * half_planes + i
-            cs_out[d, :, pl.ds(i * slab, slab)] = lax.dot_general(
-                gg[spot, :], gu[there], back, preferred_element_type=f32
-            ).astype(bf16)
-        cs_copy(d).start()
-        for i in range(half_planes):
-            mine[d, :, pl.ds(i * slab, slab)] = lax.dot_general(
-                gg[spot, :], gu[core * half_planes + i], back, preferred_element_type=f32
-            )
-
-    def slot_sum(d):
-        cs_copy(d).wait_recv()
+    chunk = width // CUTS
+    pieces = planes * CUTS
+
+    upper = (2 * z) // planes
+    near = z + upper * (planes - 1 - 2 * z)
+    far_count = planes - 1 - 2 * near
+
+    def plane_of(c):
+        i = c // CUTS
+        j = i - far_count
+        close = (j + planes) // planes
+        swing = (2 * near - j // 2) * (1 - j % 2) + (j // 2) * (j % 2)
+        d = close * swing + (1 - close) * (planes - 1 - i)
+        return d + upper * (planes - 1 - 2 * d)
+
+    def cs_copy(d, i):
+        return remote(cs_out.at[d, i], cs_in.at[d, i], cs_send.at[d, i], cs_recv.at[d, i])
+
+    def ys_copy(d, i):
+        return remote(s_out.at[d, i], comb.at[d, i, pl.ds(pair, pair), :], ys_send.at[d, i], ys_recv.at[d, i], y_peer)
+
+    def xs_copy(d, i):
+        return remote(t_out.at[d, i], xr.at[d, i], xs_send.at[d, i], xs_recv.at[d, i], x_peer)
+
+    def weight_rows(half, i):
+        start = half * width + i * chunk
+        return gu[start // slab, at(start % slab, chunk), :]
+
+    def slot_step(d, i):
+        @pl.when(i == 0)
+        def _():
+            lax.fori_loop(d * (quad // 16), (d + 1) * (quad // 16), pointwise, 0)
+
+        spot = at(d * quad, quad)
+        cs_out[d, i] = lax.dot_general(
+            gg[spot, :], weight_rows(1 - core, i), back, preferred_element_type=f32
+        ).astype(bf16)
+        cs_copy(d, i).start()
+        mine[d, i] = lax.dot_general(gg[spot, :], weight_rows(core, i), back, preferred_element_type=f32)
+
+    def slot_sum(d, i):
+        cs_copy(d, i).wait_recv()
         away, home = at((1 - y) * pair, pair), at(y * pair, pair)
-        s_out[d] = (mine[d, away, :] + cs_in[d, away, :].astype(f32)).astype(bf16)
-        ys_copy(d).start()
-        comb[d, pl.ds(0, pair), :] = (mine[d, home, :] + cs_in[d, home, :].astype(f32)).astype(bf16)
-
-    def token_step(d):
-        ys_copy(d).wait_recv()
-        t_out[d] = lax.dot_general(
-            pls[d, :, at((1 - x) * tok_rows, tok_rows)], comb[d], batch0, preferred_element_type=f32
+        s_out[d, i] = (mine[d, i, away, :] + cs_in[d, i, away, :].astype(f32)).astype(bf16)
+        ys_copy(d, i).start()
+        comb[d, i, pl.ds(0, pair), :] = (mine[d, i, home, :] + cs_in[d, i, home, :].astype(f32)).astype(bf16)
+
+    def token_step(d, i):
+        ys_copy(d, i).wait_recv()
+        t_out[d, i] = lax.dot_general(
+            pls[d, :, at((1 - x) * tok_rows, tok_rows)], comb[d, i], batch0, preferred_element_type=f32
         ).astype(bf16)
-        xs_copy(d).start()
-        t_own[d] = lax.dot_general(
-            pls[d, :, at(x * tok_rows, tok_rows)], comb[d], batch0, preferred_element_type=f32
-        )
-
-    def z_copy(d, up):
+        xs_copy(d, i).start()
+        t_own[d, i] = lax.dot_general(
+            pls[d, :, at(x * tok_rows, tok_rows)], comb[d, i], batch0, preferred_element_type=f32
+        )
+
+    def z_copy(d, i, up):
         if up:
-            return remote(z_out.at[d], z_in.at[0, d], zs_send.at[d], zs_recv.at[0, d], me + 4)
-        return remote(z_out.at[d], z_in.at[1, d], zs_send.at[d], zs_recv.at[1, d], me - 4)
-
-    def z_take(d, side):
-        remote(z_out.at[d], z_in.at[side, d], zs_send.at[d], zs_recv.at[side, d], x_peer).wait_recv()
-        t_own[d] += z_in[side, d].astype(f32)
-
-    def z_step(d):
-        xs_copy(d).wait_recv()
-        t_own[d] += xr[d].astype(f32)
-
-        @pl.when(jnp.logical_and(d > z, z > 0))
-        def _():
-            z_take(d, 0)
-
-        @pl.when(jnp.logical_and(d < z, z < planes - 1))
-        def _():
-            z_take(d, 1)
+            return remote(z_out.at[d, i], z_in.at[0, d, i], zs_send.at[d, i], zs_recv.at[0, d, i], me + 4)
+        return remote(z_out.at[d, i], z_in.at[1, d, i], zs_send.at[d, i], zs_recv.at[1, d, i], me - 4)
+
+    def z_take(d, i, side):
+        remote(
+            z_out.at[d, i], z_in.at[side, d, i], zs_send.at[d, i], zs_recv.at[side, d, i], x_peer
+        ).wait_recv()
+        t_own[d, i] += z_in[side, d, i].astype(f32)
+
+    def fin_copy(i):
+        spot = grad_tokens_ref.at[:, pl.ds(pl.multiple_of(here + i * chunk, chunk), chunk)]
+        return remote(fin.at[i], spot, fin_send.at[i], fin_recv.at[i]), pltpu.make_async_copy(
+            fin.at[i], spot, fin_keep.at[i]
+        )
+
+    def z_step(d, i):
+        xs_copy(d, i).wait_recv()
+        t_own[d, i] += xr[d, i].astype(f32)
+
+        @pl.when(jnp.logical_and(d >= z, z > 0))
+        def _():
+            z_take(d, i, 0)
+
+        @pl.when(jnp.logical_and(d <= z, z < planes - 1))
+        def _():
+            z_take(d, i, 1)
+
+        @pl.when(d != z)
+        def _():
+            z_out[d, i] = t_own[d, i].astype(bf16)
 
         @pl.when(d > z)
         def _():
-            z_out[d] = t_own[d].astype(bf16)
-            z_copy(d, True).start()
+            z_copy(d, i, True).start()
 
         @pl.when(d < z)
         def _():
-            z_out[d] = t_own[d].astype(bf16)
-            z_copy(d, False).start()
+            z_copy(d, i, False).start()
+
+        @pl.when(d == z)
+        def _():
+            fin[i] = t_own[d, i].astype(bf16)
+            out, keep = fin_copy(i)
+            out.start()
+            keep.start()
 
     tile = width // 4
 
@@ -464,64 +503,58 @@
             stage.at[w, span, :], (grad_gate_ref, grad_up_ref, grad_down_ref)[w].at[span, :], out_sem.at[w, i]
         )
 
-    def weight_grads(first, last):
-        def body(i, carry):
-            half, off, span = i // 4, at((i % 4) * tile, tile), at(i * tile, tile)
-            both = lax.dot_general(rows[0, half, :, off], gg[...], batch0, preferred_element_type=f32)
-            stage[0, span, :] = both[:, :hid].astype(bf16)
-            stage[1, span, :] = both[:, hid:].astype(bf16)
-            stage[2, span, :] = lax.dot_general(
-                rows[1, half, :, off], activ[...], batch0, preferred_element_type=f32
-            ).astype(bf16)
-            for w in range(3):
-                out_copy(w, i).start()
-            return carry
-
-        lax.fori_loop(first, last, body, 0)
-
-    order = []
-    for i in range(half_planes):
-        order += [i, planes - 1 - i]
-    for i, d in enumerate(order):
-        slot_step(d)
-        if i > 0:
-            slot_sum(order[i - 1])
-    slot_sum(order[-1])
-    weight_grads(0, 3)
-    token_step(order[0])
-    weight_grads(3, 6)
-    for i in range(1, planes):
-        token_step(order[i])
-        d = order[i - 1]
-
-        @pl.when(d != z)
-        def _():
-            z_step(d)
-
-        if i == 1:
-            weight_grads(6, 8)
-
-    @pl.when(order[-1] != z)
-    def _():
-        z_step(order[-1])
-
-    xs_copy(z).wait_recv()
-    t_own[z] += xr[z].astype(f32)
-
-    @pl.when(z > 0)
-    def _():
-        z_take(z, 0)
-
-    @pl.when(z < planes - 1)
-    def _():
-        z_take(z, 1)
-
-    fin[...] = t_own[z].astype(bf16)
-    home_spot = grad_tokens_ref.at[:, pl.ds(here, width)]
-    last = remote(fin, home_spot, fin_sem.at[0], fin_sem.at[1])
-    last.start()
-    keep = pltpu.make_async_copy(fin, home_spot, fin_sem.at[2])
-    keep.start()
+    def weight_grad(i):
+        half, off, span = i // 4, at((i % 4) * tile, tile), at(i * tile, tile)
+        both = lax.dot_general(rows[0, half, :, off], gg[...], batch0, preferred_element_type=f32)
+        stage[0, span, :] = both[:, :hid].astype(bf16)
+        stage[1, span, :] = both[:, hid:].astype(bf16)
+        stage[2, span, :] = lax.dot_general(
+            rows[1, half, :, off], activ[...], batch0, preferred_element_type=f32
+        ).astype(bf16)
+        for w in range(3):
+            out_copy(w, i).start()
+
+    def hop_lag(d):
+        waits = jnp.logical_or(jnp.logical_and(d > z, upper == 0), jnp.logical_and(d < z, upper == 1))
+        return X_LAG + jnp.where(waits, HOP_LAG * near, 0)
+
+    steps = pieces + max(8, Y_LAG + X_LAG + max(0, HOP_LAG * (planes // 2 - 1) - CUTS))
+
+    def ladder(s, carry):
+        @pl.when(s < pieces)
+        def _():
+            slot_step(plane_of(s), s % CUTS)
+
+        @pl.when(jnp.logical_and(s >= 1, s <= pieces))
+        def _():
+            slot_sum(plane_of(s - 1), (s - 1) % CUTS)
+
+        @pl.when(jnp.logical_and(s >= Y_LAG, s < pieces + Y_LAG))
+        def _():
+            token_step(plane_of(s - Y_LAG), (s - Y_LAG) % CUTS)
+
+        lag = Y_LAG + X_LAG
+
+        def z_try(c, inner):
+            d = plane_of(c)
+
+            @pl.when(c + Y_LAG + hop_lag(d) == s)
+            def _():
+                z_step(d, c % CUTS)
+
+            return inner
+
+        @pl.when(s >= lag)
+        def _():
+            lax.fori_loop(0, pieces, z_try, 0)
+
+        @pl.when(jnp.logical_and(s >= pieces, s < pieces + 8))
+        def _():
+            weight_grad(s - pieces)
+
+        return carry
+
+    lax.fori_loop(0, steps, ladder, 0)
 
     def drain_peers(k, carry):
         target = peer_of(k)
@@ -548,17 +581,18 @@
             y_copy(a, zs, y).wait_send()
             for ys in range(2):
                 core_copy(a, core, zs, ys).wait_send()
-        cs_copy(zs).wait_send()
-        ys_copy(zs).wait_send()
-        xs_copy(zs).wait_send()
-
-        @pl.when(zs > z)
-        def _():
-            z_copy(zs, True).wait_send()
-
-        @pl.when(zs < z)
-        def _():
-            z_copy(zs, False).wait_send()
+        for i in range(CUTS):
+            cs_copy(zs, i).wait_send()
+            ys_copy(zs, i).wait_send()
+            xs_copy(zs, i).wait_send()
+
+            @pl.when(zs > z)
+            def _():
+                z_copy(zs, i, True).wait_send()
+
+            @pl.when(zs < z)
+            def _():
+                z_copy(zs, i, False).wait_send()
 
         return carry
 
@@ -570,8 +604,10 @@
         return carry
 
     lax.fori_loop(0, 8, drain_out, 0)
-    keep.wait()
-    last.wait()
+    for i in range(CUTS):
+        out, keep = fin_copy(i)
+        keep.wait()
+        out.wait()
 
 
 def placed_dense(tokens, out_grad, route_ids, route_probs, gate_store, up_store, down_store):
@@ -581,6 +617,7 @@
     capacity = 9 * tok_rows * top_count // (8 * experts)
     slots, width, planes = experts * capacity, model_width // 2, experts // 4
     pair, quad, slab = 2 * capacity, 4 * capacity, model_width // planes
+    chunk = width // CUTS
     vmem, dma = pltpu.VMEM, pltpu.SemaphoreType.DMA
     anywhere, on_chip = pl.BlockSpec(memory_space=pl.ANY), pl.BlockSpec(memory_space=pltpu.VMEM)
     scratch = [
@@ -596,23 +633,24 @@
         vmem((slots, hid), f32),
         vmem((slots, hid), bf16),
         vmem((slots, 2 * hid), bf16),
-        vmem((planes, quad, width), f32),
-        vmem((planes, quad, width), bf16),
-        vmem((planes, quad, width), bf16),
-        vmem((planes, quad, width), bf16),
-        vmem((planes, pair, width), bf16),
-        vmem((planes, tok_rows, width), f32),
-        vmem((planes, tok_rows, width), bf16),
-        vmem((planes, tok_rows, width), bf16),
-        vmem((planes, tok_rows, width), bf16),
-        vmem((2, planes, tok_rows, width), bf16),
+        vmem((planes, CUTS, quad, chunk), f32),
+        vmem((planes, CUTS, quad, chunk), bf16),
+        vmem((planes, CUTS, quad, chunk), bf16),
+        vmem((planes, CUTS, quad, chunk), bf16),
+        vmem((planes, CUTS, pair, chunk), bf16),
+        vmem((planes, CUTS, tok_rows, chunk), f32),
+        vmem((planes, CUTS, tok_rows, chunk), bf16),
+        vmem((planes, CUTS, tok_rows, chunk), bf16),
+        vmem((planes, CUTS, tok_rows, chunk), bf16),
+        vmem((2, planes, CUTS, tok_rows, chunk), bf16),
         vmem((3, model_width, hid), bf16),
-        vmem((tok_rows, width), bf16),
+        vmem((CUTS, tok_rows, chunk), bf16),
         dma((2,)), dma((experts,)), dma((experts,)), dma((3, experts)), dma((3, experts)), dma((3,)),
         dma((2, planes)), dma((2, planes)), dma((2, planes)), dma((2, planes)), dma((2, planes)),
         dma((2, planes)), dma((2, planes)), dma((2, 2 * planes)), dma((2, 2 * planes)),
-        dma((planes,)), dma((planes,)), dma((planes,)), dma((planes,)),
-        dma((planes,)), dma((planes,)), dma((planes,)), dma((2, planes)), dma((3, 8)), dma((3,)),
+        dma((planes, CUTS)), dma((planes, CUTS)), dma((planes, CUTS)), dma((planes, CUTS)),
+        dma((planes, CUTS)), dma((planes, CUTS)), dma((planes, CUTS)), dma((2, planes, CUTS)),
+        dma((3, 8)), dma((CUTS,)), dma((CUTS,)), dma((CUTS,)),
     ]
     grad = jax.ShapeDtypeStruct((model_width, hid), bf16)
     outs = pl.pallas_call(

time: 209 us -> 192 us (0.919)
  Pallas kernels: 200 us -> 181 us
    pallas_call x1, Pallas kernels: 200 us -> 181 us  [placed_dense(): pl.pallas_call(functools.partial(dense_kernel, experts, capacity), out_sh...]
where the time goes in v4:
time: 192 us; the launch traced here: 189 us
  Pallas kernels  181 us (94%)
  local copies, waits for them, and re-layouts  6.99 us (4%)
    pallas_call x1, Pallas kernels, placed_dense(): pl.pallas_call(functools.partial(dense_kernel, experts, capacity), out_sh...  181 us
    unnamed x10, local copies, waits for them, and re-layouts  6.99 us

profile of v4, /device:TPU:21, one launch (start us, length us, event | category | flops | bytes accessed | tf_op | source)
XLA Modules:
  0.0 189.1 jit_solution(11622134558813854020)
XLA Ops:
  0.6 181.4 %shard_map.102 = (bf16[2048,384]{1,0:T(8,128)(2,1)}, bf16[2048,384]{1,0:T(8,128)(2,1)}, bf16[2048,384]{1,0:T(8,128)(2,1)}, bf16[128,2048]{1,0:T(8,128)(2,1)}) custom-call(s32[8,128]{1,0:T(8,128)} %bitcast.8, f32[8,128]{1,0:T(8,128)} %bitcast.9, bf16[128,2048]{1,0:T(8,128)(2,1)} %x_ref.1, bf16[128,2048]{1,0:T(8,128)(2,1)} %dy_ref.1, ...), custom_call_target="tpu_custom_call" | custom-call | tf_op jit(solution)/shard_map/pallas_call | solution.py:656
  182.1 0.0 copy-start.1
  182.1 2.8 %copy.15 = bf16[1,2048,384]{2,1,0:T(8,128)(2,1)} copy(bf16[1,2048,384]{2,1,0:T(8,128)(2,1)} %bitcast.7) | data formatting | bytes 3145728
  184.9 0.0 copy-done.1
  184.9 0.0 copy-start
  184.9 1.1 copy.16
  186.0 0.8 copy-done
  186.9 0.0 copy-start.2
  186.9 1.1 copy.17
  188.0 0.3 copy-done.2
  188.3 0.8 copy.18
Async XLA Ops:
  182.1 2.8 %copy-start.1 = (bf16[2048,384]{1,0:T(8,128)(2,1)S(1)}, bf16[2048,384]{1,0:T(8,128)(2,1)}, u32[]{:S(2)}) copy-start(bf16[2048,384]{1,0:T(8,128)(2,1)} %get-tuple-element.9) | copy-start | bytes 4718596
  184.9 2.0 %copy-start = (bf16[2048,384]{1,0:T(8,128)(2,1)S(1)}, bf16[2048,384]{1,0:T(8,128)(2,1)}, u32[]{:S(2)}) copy-start(bf16[2048,384]{1,0:T(8,128)(2,1)} %get-tuple-element.10) | copy-start | bytes 4718596
  186.9 1.4 copy-start.2

commit v5 on v4

--- a/solution.py
+++ b/solution.py
@@ -89,6 +89,8 @@
 f32, bf16 = jnp.float32, jnp.bfloat16
 MESH = pl.DeviceIdType.MESH
 CUTS = 2
+FIRST, PACE = 4, 5
+VMEM_BYTES = 56000 * 1024
 Y_LAG, X_LAG, HOP_LAG = 6, 2, 2
 
 
@@ -97,10 +99,10 @@
     ids_ref, probs_ref, x_ref, dy_ref, gate_ref, up_ref, down_ref,
     grad_gate_ref, grad_up_ref, grad_down_ref, grad_tokens_ref,
     info, info_all, gu, dn, tok, nbr_out, rows, pls, pre, act, activ, gg,
-    mine, cs_out, cs_in, comb, s_out, t_own, t_out, xr, z_out, z_in, stage, fin,
+    mine, cs_out, cs_in, comb, s_out, t_own, t_out, xr, z_out, z_in, fin,
     local_sem, info_send, info_recv, w_send, w_recv, w_own,
     ag_up, ag_down, ag_zr, ag_xs, ag_xr, y_send, y_recv, c_send, c_recv,
-    cs_send, cs_recv, ys_send, ys_recv, xs_send, xs_recv, zs_send, zs_recv, out_sem, fin_send, fin_recv, fin_keep,
+    cs_send, cs_recv, ys_send, ys_recv, xs_send, xs_recv, zs_send, zs_recv, fin_send, fin_recv, fin_keep,
 ):
     me, core = lax.axis_index("expert"), lax.axis_index("dp")
     planes = experts // 4
@@ -164,12 +166,16 @@
             src, dst = down_ref, dn.at[owner // 4, spot, :]
         return remote(src.at[target], dst, w_send.at[w, target], w_recv.at[w, owner], target)
 
-    def start_panel(w, first, last):
-        def body(k, carry):
-            w_copy(w, peer_of(k), me).start()
-            return carry
-
-        lax.fori_loop(first, last, body, 0)
+    others = experts - 1
+
+    def start_weights(first, last):
+        for w in range(3):
+
+            def body(n, carry):
+                w_copy(w, peer_of(n + 1 - w * others), me).start()
+                return carry
+
+            lax.fori_loop(jnp.maximum(first, w * others), jnp.minimum(last, (w + 1) * others), body, 0)
 
     def wait_panel(w, source):
         w_copy(w, source, source).wait_recv()
@@ -223,13 +229,15 @@
     )
     rank = jnp.dot(named.astype(bf16), jnp.where(before, 1.0, 0.0).astype(bf16), preferred_element_type=f32)
     rank = jnp.where(named > 0.5, rank + (x * capacity).astype(f32), -1.0)
-    line = lax.broadcasted_iota(jnp.int32, (experts, 8, tok_rows), 1)
-    info[...] = jnp.where(line == 0, rank[:, None, :], weight[:, None, :])
-    info_all[me] = info[at(z * 4, 4)]
+    for q in range(4):
+        for p in range(planes):
+            info[p, pl.ds(2 * q, 1), :] = rank[4 * p + q : 4 * p + q + 1, :]
+            info[p, pl.ds(2 * q + 1, 1), :] = weight[4 * p + q : 4 * p + q + 1, :]
+    info_all[me] = info[z]
 
     def info_copy(target, owner):
         return remote(
-            info.at[at((target // 4) * 4, 4)], info_all.at[owner], info_send.at[target], info_recv.at[owner], target
+            info.at[target // 4], info_all.at[owner], info_send.at[target], info_recv.at[owner], target
         )
 
     def send_info(k, carry):
@@ -237,7 +245,7 @@
         return carry
 
     lax.fori_loop(1, experts, send_info, 0)
-    start_panel(0, 1, experts)
+    start_weights(0, FIRST * others // 15)
 
     def wait_info(k, carry):
         source = peer_of(k)
@@ -251,9 +259,8 @@
 
     def places(zs, expert_index):
         first = 4 * zs + 2 * y
-        both = jnp.concatenate(
-            [info_all[first, expert_index, :, :], info_all[first + 1, expert_index, :, :]], axis=1
-        )
+        lines = pl.ds(2 * expert_index, 2)
+        both = jnp.concatenate([info_all[first, lines, :], info_all[first + 1, lines, :]], axis=1)
         hit = both[0:1, :] == lax.broadcasted_iota(jnp.int32, (pair, 2 * tok_rows), 0).astype(f32)
         prob = jnp.sum(jnp.where(hit, both[1:2, :], 0.0), axis=1, keepdims=True)
         return jnp.where(hit, 1.0, 0.0).astype(bf16), prob
@@ -289,7 +296,6 @@
         core_copy(a, core, zs, y).start()
 
     hops = 2 * planes - 2
-    others = experts - 1
 
     def spread(t, carry):
         zs, ready = walk(t), walk(t - 1)
@@ -301,42 +307,25 @@
                 remote(block, block, ag_up.at[a, zs], ag_zr.at[a, zs], x_peer).wait_recv()
                 send_block(a, zs)
 
-        @pl.when(t < planes)
-        def _():
-            start_panel(1, 1 + (t - 1) * others // (planes - 1), 1 + t * others // (planes - 1))
-
-        @pl.when(t >= planes)
-        def _():
-            start_panel(2, 1 + (t - planes) * others // planes, 1 + (t - planes + 1) * others // planes)
-
         @pl.when(inside(ready))
         def _():
             for a in range(2):
                 gather(a, ready)
 
-        return carry
-
-    def collect(a):
-        def pass_on(t, carry):
-            zs = walk(t)
-
-            @pl.when(inside(zs))
-            def _():
-                y_copy(a, zs, 1 - y).wait_recv()
-                core_copy(a, core, zs, 1 - y).start()
-
-            return carry
-
-        lax.fori_loop(0, hops + 1, pass_on, 0)
-
-        def wait_core(p, carry):
-            core_copy(a, 1 - core, p // 2, p % 2).wait_recv()
-            return carry
-
-        lax.fori_loop(0, 2 * planes, wait_core, 0)
+        start_weights((FIRST + PACE * (t - 1)) * others // 15, (FIRST + PACE * t) * others // 15)
+        return carry
 
     lax.fori_loop(1, hops + 2, spread, 0)
-    collect(0)
+    start_weights((FIRST + PACE * (hops + 1)) * others // 15, 3 * others)
+
+    def pass_on(a, zs):
+        y_copy(a, zs, 1 - y).wait_recv()
+        core_copy(a, core, zs, 1 - y).start()
+
+    def take_core(a, zs):
+        for ys in range(2):
+            core_copy(a, 1 - core, zs, ys).wait_recv()
+
     for w in range(2):
         own_panels[w].wait()
 
@@ -350,16 +339,35 @@
         half, off = (g * slab) // width, (g * slab) % width
         return rows[a, half, spot, pl.ds(off, slab)]
 
-    def forward(m, carry):
+    def forward(m):
         spot = at(m * quad, quad)
         total = jnp.dot(slab_of(0, 0, spot), gu[0], preferred_element_type=f32)
         for g in range(1, planes):
             total += jnp.dot(slab_of(0, g, spot), gu[g], preferred_element_type=f32)
         pre[spot, :] = total
-        return carry
-
-    lax.fori_loop(0, planes, forward, 0)
-    collect(1)
+
+    def first_half(t, carry):
+        zs, ready = walk(t), walk(t - 1)
+
+        @pl.when(jnp.logical_and(t <= hops, inside(zs)))
+        def _():
+            for a in range(2):
+                pass_on(a, zs)
+
+        @pl.when(jnp.logical_and(t >= 1, inside(ready)))
+        def _():
+            take_core(0, ready)
+            forward(ready)
+
+        return carry
+
+    lax.fori_loop(0, hops + 2, first_half, 0)
+
+    def settle(zs, carry):
+        take_core(1, zs)
+        return carry
+
+    lax.fori_loop(0, planes, settle, 0)
     own_panels[2].wait()
     for g in range(planes):
         for q in range(4):
@@ -497,22 +505,14 @@
 
     tile = width // 4
 
-    def out_copy(w, i):
-        span = at(i * tile, tile)
-        return pltpu.make_async_copy(
-            stage.at[w, span, :], (grad_gate_ref, grad_up_ref, grad_down_ref)[w].at[span, :], out_sem.at[w, i]
-        )
-
     def weight_grad(i):
         half, off, span = i // 4, at((i % 4) * tile, tile), at(i * tile, tile)
         both = lax.dot_general(rows[0, half, :, off], gg[...], batch0, preferred_element_type=f32)
-        stage[0, span, :] = both[:, :hid].astype(bf16)
-        stage[1, span, :] = both[:, hid:].astype(bf16)
-        stage[2, span, :] = lax.dot_general(
+        grad_gate_ref[span, :] = both[:, :hid].astype(bf16)
+        grad_up_ref[span, :] = both[:, hid:].astype(bf16)
+        grad_down_ref[span, :] = lax.dot_general(
             rows[1, half, :, off], activ[...], batch0, preferred_element_type=f32
         ).astype(bf16)
-        for w in range(3):
-            out_copy(w, i).start()
 
     def hop_lag(d):
         waits = jnp.logical_or(jnp.logical_and(d > z, upper == 0), jnp.logical_and(d < z, upper == 1))
@@ -598,12 +598,6 @@
 
     lax.fori_loop(0, planes, drain_tokens, 0)
 
-    def drain_out(i, carry):
-        for w in range(3):
-            out_copy(w, i).wait()
-        return carry
-
-    lax.fori_loop(0, 8, drain_out, 0)
     for i in range(CUTS):
         out, keep = fin_copy(i)
         keep.wait()
@@ -621,8 +615,8 @@
     vmem, dma = pltpu.VMEM, pltpu.SemaphoreType.DMA
     anywhere, on_chip = pl.BlockSpec(memory_space=pl.ANY), pl.BlockSpec(memory_space=pltpu.VMEM)
     scratch = [
+        vmem((planes, 8, tok_rows), f32),
         vmem((experts, 8, tok_rows), f32),
-        vmem((experts, 4, 8, tok_rows), f32),
         vmem((planes, slab, 2 * hid), bf16),
         vmem((planes, slab, hid), bf16),
         vmem((2, planes, 2 * tok_rows, width), bf16),
@@ -643,24 +637,23 @@
         vmem((planes, CUTS, tok_rows, chunk), bf16),
         vmem((planes, CUTS, tok_rows, chunk), bf16),
         vmem((2, planes, CUTS, tok_rows, chunk), bf16),
-        vmem((3, model_width, hid), bf16),
         vmem((CUTS, tok_rows, chunk), bf16),
         dma((2,)), dma((experts,)), dma((experts,)), dma((3, experts)), dma((3, experts)), dma((3,)),
         dma((2, planes)), dma((2, planes)), dma((2, planes)), dma((2, planes)), dma((2, planes)),
         dma((2, planes)), dma((2, planes)), dma((2, 2 * planes)), dma((2, 2 * planes)),
         dma((planes, CUTS)), dma((planes, CUTS)), dma((planes, CUTS)), dma((planes, CUTS)),
         dma((planes, CUTS)), dma((planes, CUTS)), dma((planes, CUTS)), dma((2, planes, CUTS)),
-        dma((3, 8)), dma((CUTS,)), dma((CUTS,)), dma((CUTS,)),
+        dma((CUTS,)), dma((CUTS,)), dma((CUTS,)),
     ]
-    grad = jax.ShapeDtypeStruct((model_width, hid), bf16)
+    grad = pltpu.VMEM((model_width, hid), bf16)
     outs = pl.pallas_call(
         functools.partial(dense_kernel, experts, capacity),
-        out_shape=(grad, grad, grad, jax.ShapeDtypeStruct((tok_rows, model_width), bf16)),
+        out_shape=(grad, grad, grad, pltpu.VMEM((tok_rows, model_width), bf16)),
         in_specs=[on_chip, on_chip] + [anywhere] * 5,
-        out_specs=(anywhere,) * 4,
+        out_specs=(on_chip,) * 4,
         scratch_shapes=scratch,
         compiler_params=pltpu.CompilerParams(
-            collective_id=0, has_side_effects=True, vmem_limit_bytes=60 * 1024 * 1024
+            collective_id=0, has_side_effects=True, vmem_limit_bytes=VMEM_BYTES
         ),
     )(route_ids.T, route_probs.T, tokens, out_grad, gate_store, up_store, down_store)
     return (outs[0][None], outs[1][None], outs[2][None], outs[3])

time: 192 us -> 181 us (0.943)
  Pallas kernels: 181 us -> 173 us
  local copies, waits for them, and re-layouts: 6.99 us -> 4.22 us
    pallas_call x1, Pallas kernels: 181 us -> 173 us  [placed_dense(): pl.pallas_call(functools.partial(dense_kernel, experts, capacity), out_sh...]
    unnamed x10 -> x4, local copies, waits for them, and re-layouts: 6.99 us -> 4.22 us
where the time goes in v5:
time: 181 us; the launch traced here: 178 us
  Pallas kernels  173 us (96%)
  local copies, waits for them, and re-layouts  4.22 us (2%)
    pallas_call x1, Pallas kernels, placed_dense(): pl.pallas_call(functools.partial(dense_kernel, experts, capacity), out_sh...  173 us
    unnamed x4, local copies, waits for them, and re-layouts  4.22 us

profile of v5, /device:TPU:21, one launch (start us, length us, event | category | flops | bytes accessed | tf_op | source)
XLA Modules:
  0.0 177.6 jit_solution(12051529160245523035)
XLA Ops:
  0.6 172.8 %shard_map.102 = (bf16[2048,384]{1,0:T(8,128)(2,1)S(1)}, bf16[2048,384]{1,0:T(8,128)(2,1)S(1)}, bf16[2048,384]{1,0:T(8,128)(2,1)S(1)}, bf16[128,2048]{1,0:T(8,128)(2,1)S(1)}) custom-call(s32[8,128]{1,0:T(8,128)} %bitcast.8, f32[8,128]{1,0:T(8,128)} %bitcast.9, bf16[128,2048]{1,0:T(8,128)(2,1)} %x_ref.1, bf16[128,2048]{1,0:T(8,128)(2,1)} %dy_ref.1, ...), custom_call_target="tpu_custom_call" | custom-call | tf_op jit(solution)/shard_map/pallas_call | solution.py:649
  173.4 1.1 copy.15
  174.6 1.1 copy.16
  175.7 0.8 copy.18
  176.5 1.1 copy.17

commit v6 on v5

--- a/solution.py
+++ b/solution.py
@@ -89,6 +89,7 @@
 f32, bf16 = jnp.float32, jnp.bfloat16
 MESH = pl.DeviceIdType.MESH
 CUTS = 2
+S_LAG = 3
 FIRST, PACE = 4, 5
 VMEM_BYTES = 56000 * 1024
 Y_LAG, X_LAG, HOP_LAG = 6, 2, 2
@@ -228,7 +229,7 @@
         jnp.int32, (tok_rows, tok_rows), 1
     )
     rank = jnp.dot(named.astype(bf16), jnp.where(before, 1.0, 0.0).astype(bf16), preferred_element_type=f32)
-    rank = jnp.where(named > 0.5, rank + (x * capacity).astype(f32), -1.0)
+    rank = jnp.where(named > 0.5, rank, -4.0 * capacity)
     for q in range(4):
         for p in range(planes):
             info[p, pl.ds(2 * q, 1), :] = rank[4 * p + q : 4 * p + q + 1, :]
@@ -257,12 +258,13 @@
     def pair_rows(zs, ys):
         return at((2 * zs + ys) * pair, pair)
 
-    def places(zs, expert_index):
-        first = 4 * zs + 2 * y
+    def places(first, second, expert_index):
         lines = pl.ds(2 * expert_index, 2)
-        both = jnp.concatenate([info_all[first, lines, :], info_all[first + 1, lines, :]], axis=1)
-        hit = both[0:1, :] == lax.broadcasted_iota(jnp.int32, (pair, 2 * tok_rows), 0).astype(f32)
-        prob = jnp.sum(jnp.where(hit, both[1:2, :], 0.0), axis=1, keepdims=True)
+        one, two = info_all[first, lines, :], info_all[second, lines, :]
+        ranks = jnp.concatenate([one[0:1, :], two[0:1, :] + float(capacity)], axis=1)
+        probs = jnp.concatenate([one[1:2, :], two[1:2, :]], axis=1)
+        hit = ranks == lax.broadcasted_iota(jnp.int32, (pair, 2 * tok_rows), 0).astype(f32)
+        prob = jnp.sum(jnp.where(hit, probs, 0.0), axis=1, keepdims=True)
         return jnp.where(hit, 1.0, 0.0).astype(bf16), prob
 
     def y_copy(a, zs, ys):
@@ -278,11 +280,14 @@
     peer_q = y_peer % 4
 
     def gather(a, zs):
-        own_place, own_prob = places(zs, mine_q)
-        nbr_place, nbr_prob = places(zs, peer_q)
+        first = 4 * zs + 2 * y
+        own_place, own_prob = places(first, first + 1, mine_q)
+        nbr_place, nbr_prob = places(first, first + 1, peer_q)
         if a == 0:
-            pls[zs, pl.ds(0, pair), :] = own_place
-            pls[zs, pl.ds(pair, pair), :] = nbr_place
+            pls[0, zs, pl.ds(0, pair), :] = own_place
+            pls[0, zs, pl.ds(pair, pair), :] = nbr_place
+            for k, q in enumerate((mine_q, x_peer % 4)):
+                pls[1, zs, pl.ds(k * pair, pair), :] = places(4 * zs + x, 4 * zs + 2 + x, q)[0]
         ag_copy(a, zs, 2).wait_recv()
         lent = jnp.dot(nbr_place, tok[a, zs], preferred_element_type=f32)
         if a == 1:
@@ -413,14 +418,19 @@
         d = close * swing + (1 - close) * (planes - 1 - i)
         return d + upper * (planes - 1 - 2 * d)
 
+    def blend(i, first, second):
+        return first + (second - first) * i
+
     def cs_copy(d, i):
         return remote(cs_out.at[d, i], cs_in.at[d, i], cs_send.at[d, i], cs_recv.at[d, i])
 
     def ys_copy(d, i):
-        return remote(s_out.at[d, i], comb.at[d, i, pl.ds(pair, pair), :], ys_send.at[d, i], ys_recv.at[d, i], y_peer)
+        return remote(
+            s_out.at[d, i], comb.at[d, i, pl.ds(pair, pair), :], ys_send.at[d, i], ys_recv.at[d, i], blend(i, y_peer, x_peer)
+        )
 
     def xs_copy(d, i):
-        return remote(t_out.at[d, i], xr.at[d, i], xs_send.at[d, i], xs_recv.at[d, i], x_peer)
+        return remote(t_out.at[d, i], xr.at[d, i], xs_send.at[d, i], xs_recv.at[d, i], blend(i, x_peer, y_peer))
 
     def weight_rows(half, i):
         start = half * width + i * chunk
@@ -440,19 +450,26 @@
 
     def slot_sum(d, i):
         cs_copy(d, i).wait_recv()
-        away, home = at((1 - y) * pair, pair), at(y * pair, pair)
-        s_out[d, i] = (mine[d, i, away, :] + cs_in[d, i, away, :].astype(f32)).astype(bf16)
+        mine[d, i] += cs_in[d, i].astype(f32)
+
+        def both(q):
+            return jnp.concatenate(
+                [mine[d, i, at(q * capacity, capacity), :], mine[d, i, at((q + 1 + i) * capacity, capacity), :]], axis=0
+            ).astype(bf16)
+
+        s_out[d, i] = both(blend(i, 2 - 2 * y, 1 - x))
         ys_copy(d, i).start()
-        comb[d, i, pl.ds(0, pair), :] = (mine[d, i, home, :] + cs_in[d, i, home, :].astype(f32)).astype(bf16)
+        comb[d, i, pl.ds(0, pair), :] = both(blend(i, 2 * y, x))
 
     def token_step(d, i):
         ys_copy(d, i).wait_recv()
+        here_first = blend(i, x, y)
         t_out[d, i] = lax.dot_general(
-            pls[d, :, at((1 - x) * tok_rows, tok_rows)], comb[d, i], batch0, preferred_element_type=f32
+            pls[i, d, :, at((1 - here_first) * tok_rows, tok_rows)], comb[d, i], batch0, preferred_element_type=f32
         ).astype(bf16)
         xs_copy(d, i).start()
         t_own[d, i] = lax.dot_general(
-            pls[d, :, at(x * tok_rows, tok_rows)], comb[d, i], batch0, preferred_element_type=f32
+            pls[i, d, :, at(here_first * tok_rows, tok_rows)], comb[d, i], batch0, preferred_element_type=f32
         )
 
     def z_copy(d, i, up):
@@ -525,13 +542,17 @@
         def _():
             slot_step(plane_of(s), s % CUTS)
 
-        @pl.when(jnp.logical_and(s >= 1, s <= pieces))
+        @pl.when(jnp.logical_and(s >= 1, s <= 2 * CUTS))
         def _():
             slot_sum(plane_of(s - 1), (s - 1) % CUTS)
 
         @pl.when(jnp.logical_and(s >= Y_LAG, s < pieces + Y_LAG))
         def _():
             token_step(plane_of(s - Y_LAG), (s - Y_LAG) % CUTS)
+
+        @pl.when(jnp.logical_and(s > 2 * CUTS + S_LAG, s <= pieces + S_LAG))
+        def _():
+            slot_sum(plane_of(s - 1 - S_LAG), (s - 1 - S_LAG) % CUTS)
 
         lag = Y_LAG + X_LAG
 
@@ -622,7 +643,7 @@
         vmem((2, planes, 2 * tok_rows, width), bf16),
         vmem((2, planes, pair, width), bf16),
         vmem((2, 2, slots, width), bf16),
-        vmem((planes, quad, 2 * tok_rows), bf16),
+        vmem((2, planes, quad, 2 * tok_rows), bf16),
         vmem((slots, 2 * hid), f32),
         vmem((slots, hid), f32),
         vmem((slots, hid), bf16),

time: 181 us -> 180 us (level); the launches traced: 178 us -> 179 us
  no operation moved by 1% of the time
where the time goes in v6:
time: 180 us; the launch traced here: 179 us
  Pallas kernels  174 us (97%)
  local copies, waits for them, and re-layouts  4.22 us (2%)
    pallas_call x1, Pallas kernels, placed_dense(): pl.pallas_call(functools.partial(dense_kernel, experts, capacity), out_sh...  174 us
    unnamed x4, local copies, waits for them, and re-layouts  4.22 us

profile of v6, /device:TPU:21, one launch (start us, length us, event | category | flops | bytes accessed | tf_op | source)
XLA Modules:
  0.0 179.3 jit_solution(16400025524277802071)
XLA Ops:
  0.6 174.4 %shard_map.102 = (bf16[2048,384]{1,0:T(8,128)(2,1)S(1)}, bf16[2048,384]{1,0:T(8,128)(2,1)S(1)}, bf16[2048,384]{1,0:T(8,128)(2,1)S(1)}, bf16[128,2048]{1,0:T(8,128)(2,1)S(1)}) custom-call(s32[8,128]{1,0:T(8,128)} %bitcast.8, f32[8,128]{1,0:T(8,128)} %bitcast.9, bf16[128,2048]{1,0:T(8,128)(2,1)} %x_ref.1, bf16[128,2048]{1,0:T(8,128)(2,1)} %dy_ref.1, ...), custom_call_target="tpu_custom_call" | custom-call | tf_op jit(solution)/shard_map/pallas_call | solution.py:670
  175.1 1.1 copy.15
  176.2 1.1 copy.16
  177.3 0.8 copy.18
  178.1 1.1 copy.17

commit v7 on v6

--- a/solution.py
+++ b/solution.py
@@ -374,7 +374,9 @@
 
     lax.fori_loop(0, planes, settle, 0)
     own_panels[2].wait()
-    for g in range(planes):
+    upper = (2 * z) // planes
+    for turn in range(planes):
+        g = turn + upper * (planes - 1 - 2 * turn)
         for q in range(4):
             source = 4 * g + q
 
@@ -384,8 +386,8 @@
 
         def backward(m, carry):
             spot = at(m * quad, quad)
-            part = jnp.dot(slab_of(1, g, spot), dn[g], preferred_element_type=f32)
-            if g == 0:
+            part = jnp.dot(rows[1, (g * slab) // width, spot, at((g * slab) % width, slab)], dn[g], preferred_element_type=f32)
+            if turn == 0:
                 act[spot, :] = part
             else:
                 act[spot, :] += part
@@ -406,7 +408,6 @@
     chunk = width // CUTS
     pieces = planes * CUTS
 
-    upper = (2 * z) // planes
     near = z + upper * (planes - 1 - 2 * z)
     far_count = planes - 1 - 2 * near
 

time: 180 us -> 179 us (level)
  no operation moved by 1% of the time
where the time goes in v7:
time: 179 us
  Pallas kernels  174 us (97%)
  local copies, waits for them, and re-layouts  4.22 us (2%)
    pallas_call x1, Pallas kernels, placed_dense(): pl.pallas_call(functools.partial(dense_kernel, experts, capacity), out_sh...  174 us
    unnamed x4, local copies, waits for them, and re-layouts  4.22 us

profile of v7, /device:TPU:21, one launch (start us, length us, event | category | flops | bytes accessed | tf_op | source)
XLA Modules:
  0.0 178.7 jit_solution(6920823748947708811)
XLA Ops:
  0.6 173.8 %shard_map.102 = (bf16[2048,384]{1,0:T(8,128)(2,1)S(1)}, bf16[2048,384]{1,0:T(8,128)(2,1)S(1)}, bf16[2048,384]{1,0:T(8,128)(2,1)S(1)}, bf16[128,2048]{1,0:T(8,128)(2,1)S(1)}) custom-call(s32[8,128]{1,0:T(8,128)} %bitcast.8, f32[8,128]{1,0:T(8,128)} %bitcast.9, bf16[128,2048]{1,0:T(8,128)(2,1)} %x_ref.1, bf16[128,2048]{1,0:T(8,128)(2,1)} %dy_ref.1, ...), custom_call_target="tpu_custom_call" | custom-call | tf_op jit(solution)/shard_map/pallas_call | solution.py:671
  174.4 1.1 copy.15
  175.6 1.1 copy.16
  176.7 0.8 copy.18
  177.5 1.1 copy.17

commit v8 on v7

--- a/solution.py
+++ b/solution.py
@@ -155,72 +155,6 @@
         copy.start()
     for copy in own_panels:
         copy.start()
-    pl.semaphore_wait(barrier, experts)
-
-    def w_copy(w, target, owner):
-        spot = at((owner % 4) * tok_rows, tok_rows)
-        if w == 0:
-            src, dst = gate_ref, gu.at[owner // 4, spot, pl.ds(0, hid)]
-        elif w == 1:
-            src, dst = up_ref, gu.at[owner // 4, spot, pl.ds(hid, hid)]
-        else:
-            src, dst = down_ref, dn.at[owner // 4, spot, :]
-        return remote(src.at[target], dst, w_send.at[w, target], w_recv.at[w, owner], target)
-
-    others = experts - 1
-
-    def start_weights(first, last):
-        for w in range(3):
-
-            def body(n, carry):
-                w_copy(w, peer_of(n + 1 - w * others), me).start()
-                return carry
-
-            lax.fori_loop(jnp.maximum(first, w * others), jnp.minimum(last, (w + 1) * others), body, 0)
-
-    def wait_panel(w, source):
-        w_copy(w, source, source).wait_recv()
-
-    def tok_block(a, zs, xs):
-        return tok.at[a, zs, at(xs * tok_rows, tok_rows), :]
-
-    def ag_copy(a, zs, direction):
-        block = tok_block(a, zs, x)
-        if direction == 0:
-            return remote(block, block, ag_up.at[a, zs], ag_zr.at[a, zs], me + 4)
-        if direction == 1:
-            return remote(block, block, ag_down.at[a, zs], ag_zr.at[a, zs], me - 4)
-        return remote(block, block, ag_xs.at[a, zs], ag_xr.at[a, zs], x_peer)
-
-    def walk(t):
-        return z + ((t + 1) // 2) * (1 - 2 * (t % 2))
-
-    def inside(zs):
-        return jnp.logical_and(zs >= 0, zs < planes)
-
-    def forwards(zs):
-        return (
-            jnp.logical_and(zs <= z, z < planes - 1),
-            jnp.logical_and(zs >= z, z > 0),
-        )
-
-    def send_block(a, zs):
-        go_up, go_down = forwards(zs)
-
-        @pl.when(go_up)
-        def _():
-            ag_copy(a, zs, 0).start()
-
-        @pl.when(go_down)
-        def _():
-            ag_copy(a, zs, 1).start()
-
-        ag_copy(a, zs, 2).start()
-
-    for a in range(2):
-        own_copies[a].wait()
-        send_block(a, z)
-
     ids, probs = ids_ref[...], probs_ref[...]
     named_by = lax.broadcasted_iota(jnp.int32, (experts,) + ids.shape, 0) == ids[None, :, :]
     weight = jnp.sum(jnp.where(named_by, probs[None, :, :], 0.0), axis=1)
@@ -235,6 +169,72 @@
             info[p, pl.ds(2 * q, 1), :] = rank[4 * p + q : 4 * p + q + 1, :]
             info[p, pl.ds(2 * q + 1, 1), :] = weight[4 * p + q : 4 * p + q + 1, :]
     info_all[me] = info[z]
+
+    pl.semaphore_wait(barrier, experts)
+
+    def w_copy(w, target, owner):
+        spot = at((owner % 4) * tok_rows, tok_rows)
+        if w == 0:
+            src, dst = gate_ref, gu.at[owner // 4, spot, pl.ds(0, hid)]
+        elif w == 1:
+            src, dst = up_ref, gu.at[owner // 4, spot, pl.ds(hid, hid)]
+        else:
+            src, dst = down_ref, dn.at[owner // 4, spot, :]
+        return remote(src.at[target], dst, w_send.at[w, target], w_recv.at[w, owner], target)
+
+    others = experts - 1
+
+    def start_weights(first, last):
+        for w in range(3):
+
+            def body(n, carry):
+                w_copy(w, peer_of(n + 1 - w * others), me).start()
+                return carry
+
+            lax.fori_loop(jnp.maximum(first, w * others), jnp.minimum(last, (w + 1) * others), body, 0)
+
+    def wait_panel(w, source):
+        w_copy(w, source, source).wait_recv()
+
+    def tok_block(a, zs, xs):
+        return tok.at[a, zs, at(xs * tok_rows, tok_rows), :]
+
+    def ag_copy(a, zs, direction):
+        block = tok_block(a, zs, x)
+        if direction == 0:
+            return remote(block, block, ag_up.at[a, zs], ag_zr.at[a, zs], me + 4)
+        if direction == 1:
+            return remote(block, block, ag_down.at[a, zs], ag_zr.at[a, zs], me - 4)
+        return remote(block, block, ag_xs.at[a, zs], ag_xr.at[a, zs], x_peer)
+
+    def walk(t):
+        return z + ((t + 1) // 2) * (1 - 2 * (t % 2))
+
+    def inside(zs):
+        return jnp.logical_and(zs >= 0, zs < planes)
+
+    def forwards(zs):
+        return (
+            jnp.logical_and(zs <= z, z < planes - 1),
+            jnp.logical_and(zs >= z, z > 0),
+        )
+
+    def send_block(a, zs):
+        go_up, go_down = forwards(zs)
+
+        @pl.when(go_up)
+        def _():
+            ag_copy(a, zs, 0).start()
+
+        @pl.when(go_down)
+        def _():
+            ag_copy(a, zs, 1).start()
+
+        ag_copy(a, zs, 2).start()
+
+    for a in range(2):
+        own_copies[a].wait()
+        send_block(a, z)
 
     def info_copy(target, owner):
         return remote(

time: 179 us -> 179 us (level)
  no operation moved by 1% of the time
where the time goes in v8:
time: 179 us
  Pallas kernels  174 us (97%)
  local copies, waits for them, and re-layouts  4.22 us (2%)
    pallas_call x1, Pallas kernels, placed_dense(): pl.pallas_call(functools.partial(dense_kernel, experts, capacity), out_sh...  174 us
    unnamed x4, local copies, waits for them, and re-layouts  4.22 us

profile of v8, /device:TPU:21, one launch (start us, length us, event | category | flops | bytes accessed | tf_op | source)
XLA Modules:
  0.0 178.7 jit_solution(1214225890784759406)
XLA Ops:
  0.6 173.8 %shard_map.102 = (bf16[2048,384]{1,0:T(8,128)(2,1)S(1)}, bf16[2048,384]{1,0:T(8,128)(2,1)S(1)}, bf16[2048,384]{1,0:T(8,128)(2,1)S(1)}, bf16[128,2048]{1,0:T(8,128)(2,1)S(1)}) custom-call(s32[8,128]{1,0:T(8,128)} %bitcast.8, f32[8,128]{1,0:T(8,128)} %bitcast.9, bf16[128,2048]{1,0:T(8,128)(2,1)} %x_ref.1, bf16[128,2048]{1,0:T(8,128)(2,1)} %dy_ref.1, ...), custom_call_target="tpu_custom_call" | custom-call | tf_op jit(solution)/shard_map/pallas_call | solution.py:671
  174.4 1.1 copy.15
  175.6 1.1 copy.16
  176.7 0.8 copy.18
  177.5 1.1 copy.17
